TPU v7x, 256 devices: a whole 4x4x8 slice. The times are simulated.
256 devices in a mesh: inst: 16 (over x, y_lo, core), space: 16 (over z, y_hi).
Axes of the slice: x: 4, y: 4 (y_hi: 2, y_lo: 2; y = y_hi * 2 + y_lo), z: 8, core: 2. Of those that a mesh axis runs over, the one named last changes fastest.
Arguments:
- adjoint: float32 [16, 5, 64, 16, 128], P('inst', None, 'space'), may hold values from -6 to 6
- jacobian: float32 [16, 7, 5, 5, 64, 16, 128], P('inst', None, None, None, 'space'), may hold values from -4 to 4
- volume: float32 [64, 16, 128], P('space'), may hold values from 0.5 to 2
- source: float32 [16, 5, 64, 16, 128], P('inst', None, 'space'), may hold values from -6 to 6
- surface_out: float32 [5, 64, 128], P(None, 'space'), may hold values from -0.5 to 0.5
- surface_in: float32 [5, 64, 128], P(None, 'space'), may hold values from -6 to 6
- station: int32 [64, 128], P('space'), may hold values from 0 to 255
- phi: float32 [40, 256], replicated, may hold values from -0.375 to 0.375
- inv_stiff: float32 [40], replicated, may hold values from 0.5 to 8
Outputs:
- residual: float32 [16, 5, 64, 16, 128], P('inst', None, 'space')
- modal: float32 [16, 40], P('inst')
All inputs are finite; a program needn't handle non-finite values.
Results may differ from a plain program's by a relative error of at most 0.000078.
Values sent between devices are 32-bit elements; how exact they have to be, the bound alone decides.
A program may use at most 64 MiB of HBM per device.

v0:
```python
import jax
import jax.numpy as jnp
from jax import lax
from jax.sharding import PartitionSpec as P


def padded(cells, sides, width):
    for axis, dim in sides:
        count = lax.axis_size(axis)
        head = lax.slice_in_dim(cells, 0, width, axis=dim)
        tail = lax.slice_in_dim(cells, cells.shape[dim] - width, cells.shape[dim], axis=dim)
        cells = jnp.concatenate(
            [
                lax.ppermute(tail, axis, [(i, (i + 1) % count) for i in range(count)]),
                cells,
                lax.ppermute(head, axis, [((i + 1) % count, i) for i in range(count)]),
            ],
            axis=dim,
        )
    return cells


def time_weights(count):
    index = jnp.arange(count)
    diff = index[:, None] - index[None, :]
    angle = jnp.pi * diff.astype(jnp.float32) / count
    parity = (1 - 2 * (diff % 2)).astype(jnp.float32)
    offdiag = diff != 0
    safe_sin = jnp.where(offdiag, jnp.sin(angle), jnp.float32(1.0))
    first = jnp.where(offdiag, 0.5 * parity * jnp.cos(angle) / safe_sin, jnp.float32(0.0))
    second = jnp.where(offdiag, -0.5 * parity / (safe_sin * safe_sin), -(count * count + 2) / 12.0)
    return first - 0.25 * second


def body(adjoint, jacobian, volume, source, surface_out, surface_in, station, phi, inv_stiff):
    lam = adjoint[0]
    count = lax.axis_size("inst")
    weights = time_weights(count)
    my_inst = lax.axis_index("inst")
    column = weights[:, my_inst]
    mixed = jnp.einsum(
        "m,mjxyz->jxyz",
        column,
        lax.all_gather(adjoint, "inst", axis=0, tiled=True),
        precision=lax.Precision.HIGHEST,
    )
    spectral = volume[None] * mixed
    face = jnp.sum(surface_out * lam[:, :, 0, :], axis=0)
    stations = phi.shape[1]
    onehot = (station.reshape(-1)[:, None] == jnp.arange(stations)[None, :]).astype(jnp.float32)
    local_loads = jnp.dot(face.reshape(-1), onehot, precision=lax.Precision.HIGHEST)
    loads = lax.psum(local_loads, "space")
    modal = inv_stiff * jnp.dot(phi, loads, precision=lax.Precision.HIGHEST)
    prod = jnp.einsum("dijxyz,ixyz->djxyz", jacobian[0], lam, precision=lax.Precision.HIGHEST)
    extended = padded(jnp.stack([prod[1], prod[2]]), (("space", 2),), 1)
    from_left = extended[0][:, :-2]
    from_right = extended[1][:, 2:]
    flux = prod[0] + from_left + from_right
    flux = flux + jnp.pad(prod[3], ((0, 0), (0, 0), (1, 0), (0, 0)))[:, :, :-1]
    flux = flux + jnp.pad(prod[4], ((0, 0), (0, 0), (0, 1), (0, 0)))[:, :, 1:]
    flux = flux + jnp.pad(prod[5], ((0, 0), (0, 0), (0, 0), (1, 0)))[:, :, :, :-1]
    flux = flux + jnp.pad(prod[6], ((0, 0), (0, 0), (0, 0), (0, 1)))[:, :, :, 1:]
    face_modes = jnp.dot(onehot, phi.T, precision=lax.Precision.HIGHEST)
    back = jnp.dot(face_modes, modal, precision=lax.Precision.HIGHEST).reshape(face.shape)
    residual = flux + spectral - source[0]
    residual = residual.at[:, :, 0, :].add(surface_in * back[None])
    return (residual[None], modal[None])


def solution(mesh):
    placed = (
        P("inst", None, "space", None, None),
        P("inst", None, None, None, "space", None, None),
        P("space", None, None),
        P("inst", None, "space", None, None),
        P(None, "space", None),
        P(None, "space", None),
        P("space", None),
        P(),
        P(),
    )
    return jax.shard_map(
        body,
        mesh=mesh,
        in_specs=placed,
        out_specs=(P("inst", None, "space", None, None), P("inst", None)),
        check_vma=False,
    )
```

profile of v0, /device:TPU:6, one launch (start us, length us, event | category | flops | bytes accessed | tf_op | source)
XLA Modules:
  0.0 76.4 jit_solution(7503859074417979905)
XLA Ops:
  7.2 0.0 copy-start
  7.2 0.0 all-gather.2.cloned.1.call-start
  7.2 0.7 all-gather.2.cloned.1.call-update
  7.9 1.0 %copy.41 = f32[1,5,4,16,128]{4,2,1,3,0:T(4,128)S(1)} copy(f32[1,5,4,16,128]{4,3,2,1,0:T(8,128)} %param.11) | data formatting | bytes 327680
  8.9 3.5 %fusion = f32[4,16,128,7,5]{2,1,0,4,3:T(8,128)S(1)} fusion(f32[1,7,5,5,4,16,128]{6,5,4,3,2,1,0:T(8,128)} %param.12, f32[4,16,128,5]{2,1,0,3:T(8,128)S(1)} %copy.31), kind=kLoop, calls=%fused_computation.1 | loop fusion | flops 2580480 | bytes 7045120
  12.5 0.0 copy-start.4
  12.5 0.4 copy.40
  13.0 0.1 fusion.54
  13.1 3.3 %collective-permute-start = (f32[2,5,1,16,128]{4,2,1,3,0:T(1,128)S(1)}, f32[2,5,1,16,128]{4,2,1,3,0:T(1,128)S(1)}, u32[]{:S(2)}, u32[]{:S(2)}) collective-permute-start(f32[2,5,1,16,128]{4,2,1,3,0:T(1,128)S(1)} %get-tuple-element.14), channel_id=1, source_target_pairs={{0,1},{1,2},{2,3},{3,4},{4,5},{5,6},{6,7},{7,8},{8,9},{9,10},{10,1... | collective-permute-start | bytes 245768 | tf_op jit(solution)/shard_map/ppermute | solution.py:14
  16.4 5.4 %collective-permute-start.1 = (f32[2,5,1,16,128]{4,2,1,3,0:T(1,128)S(1)}, f32[2,5,1,16,128]{4,2,1,3,0:T(1,128)S(1)}, u32[]{:S(2)}, u32[]{:S(2)}) collective-permute-start(f32[2,5,1,16,128]{4,2,1,3,0:T(1,128)S(1)} %get-tuple-element.15), channel_id=1, source_target_pairs={{1,0},{2,1},{3,2},{4,3},{5,4},{6,5},{7,6},{8,7},{9,8},{10,9},{11,1... | collective-permute-start | bytes 245768 | tf_op jit(solution)/shard_map/ppermute | solution.py:16
  21.8 0.3 fusion.4
  22.1 40.4 %psum.7 = f32[256]{0:T(256)S(1)} all-reduce(f32[256]{0:T(256)S(1)} %bitcast.91), channel_id=1, replica_groups=mesh['inst'=16,'space'=16] {'space'}, use_global_device_ids=true, to_apply=%region_1.2 | all-reduce | flops 256 | bytes 2048 | tf_op jit(solution)/shard_map/psum | solution.py:52
  62.5 0.1 convert_multiply_fusion
  62.6 0.1 fusion.3
  62.7 0.4 fusion.5
  63.2 0.3 fusion.30
  63.5 0.1 slice_bitcast_fusion.2
  63.7 0.2 pad_maximum_fusion
  64.0 0.0 all-gather.2.cloned.1.call-done
  64.0 4.4 %fusion.1 = f32[1,5,4,16,128]{4,0,3,2,1:T(1,128)S(1)} fusion(f32[16,5,4,16,128]{4,3,2,1,0:T(8,128)} %all-gather.2.cloned.1.call-done, pred[16,16]{0,1:T(8,128)(4,1)S(1)} %fusion.19, s32[]{:T(128)S(6)} %select_n.25, f32[16,16]{0,1:T(8,128)S(1)} %get-tuple-element.24, f32[16,16]{0,1:T(8,128)S(1)} %get-tuple-element.25, s32[16,16]{0,1:T(8,128)S(1)} %fusion.18), kind=kOutput, calls=%fused_computation.2 | convolution fusion | flops 7864512 | bytes 2787332 | tf_op jit(solution)/shard_map/m,mjxyz->jxyz/dot_general | solution.py:41
  68.5 0.3 fusion.13
  68.8 0.1 scatter-add.4
  68.9 0.0 copy-start.2
  68.9 0.7 copy-done.2
  (25 shorter events, 0.2 us)
Async XLA Ops:
  7.2 55.4 %copy-start = (f32[40,256]{1,0:T(8,128)S(1)}, f32[40,256]{1,0:T(8,128)}, u32[]{:S(2)}) copy-start(f32[40,256]{1,0:T(8,128)} %param.18) | copy-start | bytes 122884
  7.2 56.8 %all-gather.2.cloned.1.call-start = ((), (), s32[]{:S(2)}) async-start(), calls=%async_computation | async-start | bytes 2785280 | tf_op jit(solution)/shard_map/all_gather | solution.py:44
  12.5 9.3 %copy-start.3 = (f32[4,16,128]{2,1,0:T(8,128)S(1)}, f32[4,16,128]{2,1,0:T(8,128)}, u32[]{:S(2)}) copy-start(f32[4,16,128]{2,1,0:T(8,128)} %param.13) | copy-start | bytes 98308
  12.5 9.4 %copy-start.4 = (f32[5,4,128]{2,1,0:T(4,128)S(1)}, f32[5,4,128]{2,1,0:T(4,128)}, u32[]{:S(2)}) copy-start(f32[5,4,128]{2,1,0:T(4,128)} %param.15) | copy-start | bytes 30724
  12.5 9.4 %copy-start.6 = (s32[4,128]{1,0:T(4,128)S(1)}, s32[4,128]{1,0:T(4,128)}, u32[]{:S(2)}) copy-start(s32[4,128]{1,0:T(4,128)} %param.17) | copy-start | bytes 6148
  12.5 50.1 %copy-start.8 = (f32[40]{0:T(128)S(1)}, f32[40]{0:T(128)}, u32[]{:S(2)}) copy-start(f32[40]{0:T(128)} %param.19) | copy-start | bytes 484
  13.1 50.6 %collective-permute-start = (f32[2,5,1,16,128]{4,2,1,3,0:T(1,128)S(1)}, f32[2,5,1,16,128]{4,2,1,3,0:T(1,128)S(1)}, u32[]{:S(2)}, u32[]{:S(2)}) collective-permute-start(f32[2,5,1,16,128]{4,2,1,3,0:T(1,128)S(1)} %get-tuple-element.14), channel_id=1, source_target_pairs={{0,1},{1,2},{2,3},{3,4},{4,5},{5,6},{6,7},{7,8},{8,9},{9,10},{10,1... | collective-permute-start | bytes 245768 | tf_op jit(solution)/shard_map/ppermute | solution.py:14
  16.4 47.3 %collective-permute-start.1 = (f32[2,5,1,16,128]{4,2,1,3,0:T(1,128)S(1)}, f32[2,5,1,16,128]{4,2,1,3,0:T(1,128)S(1)}, u32[]{:S(2)}, u32[]{:S(2)}) collective-permute-start(f32[2,5,1,16,128]{4,2,1,3,0:T(1,128)S(1)} %get-tuple-element.15), channel_id=1, source_target_pairs={{1,0},{2,1},{3,2},{4,3},{5,4},{6,5},{7,6},{8,7},{9,8},{10,9},{11,1... | collective-permute-start | bytes 245768 | tf_op jit(solution)/shard_map/ppermute | solution.py:16
  62.7 5.7 %copy-start.7 = (f32[40]{0:T(128)}, f32[40]{0:T(128)S(1)}, u32[]{:S(2)}) copy-start(f32[40]{0:T(128)S(1)} %fusion.3) | copy-start | bytes 484
  63.6 4.8 %copy-start.1 = (f32[1,5,4,16,128]{4,3,2,1,0:T(8,128)S(1)}, f32[1,5,4,16,128]{4,3,2,1,0:T(8,128)}, u32[]{:S(2)}) copy-start(f32[1,5,4,16,128]{4,3,2,1,0:T(8,128)} %param.14) | copy-start | bytes 491524
  63.9 4.8 %copy-start.5 = (f32[5,4,128]{2,1,0:T(4,128)S(1)}, f32[5,4,128]{2,1,0:T(4,128)}, u32[]{:S(2)}) copy-start(f32[5,4,128]{2,1,0:T(4,128)} %param.16) | copy-start | bytes 30724
  68.9 0.7 copy-start.2
Sparse Core Ops, SparseCore 0:
  9.9 39.5 all-gather.1
where the time goes:
time: 76.6 us; the launch traced here: 76.4 us
  blocking collectives  40.4 us (53%)
  between operations  14.3 us (19%)
  starting transfers between devices  8.69 us (11%)
  matrix products  5.64 us (7%)
  other arithmetic  4.13 us (5%)
  local copies, waits for them, and re-layouts  2.52 us (3%)
    psum x1, blocking collectives, body(): loads = lax.psum(local_loads, 'space')  40.4 us
    ppermute x1, starting transfers between devices, padded(): lax.ppermute(head, axis, [((i + 1) % count, i) for i in range(count)])  5.38 us
    dot_general x1, matrix products, body(): jnp.einsum('m,mjxyz->jxyz', column, lax.all_gather(adjoint, 'inst', axis=...  4.45 us
    unnamed x1, other arithmetic  3.53 us
    ppermute x1, starting transfers between devices, padded(): lax.ppermute(tail, axis, [(i, (i + 1) % count) for i in range(count)])  3.27 us
    unnamed x21, local copies, waits for them, and re-layouts  1.72 us
  transfers between devices with their start and end apart: 3, of which 0 were waited for; matrix products, arithmetic and copies ran while one was open for 9% of the time, Pallas kernels for 0%

commit v1 on v0

v1 whole, which is shorter than its diff:
```python
import functools

import numpy as np
import jax
import jax.numpy as jnp
from jax import lax
from jax.experimental import pallas as pl
from jax.experimental.pallas import tpu as pltpu
from jax.sharding import PartitionSpec as P

MESH = pl.DeviceIdType.MESH
FIRST = (0, 3)
COUNT = (3, 2)


def time_weight(count):
    k = np.arange(count)
    angle = np.pi * k / count
    parity = 1.0 - 2.0 * (k % 2)
    safe = np.where(k != 0, np.sin(angle), 1.0)
    first = np.where(k != 0, 0.5 * parity * np.cos(angle) / safe, 0.0)
    second = np.where(k != 0, -0.5 * parity / (safe * safe), -(count * count + 2) / 12.0)
    return first - 0.25 * second


def kernel(
    ni, ns,
    adj_hbm, jac_hbm, vol_hbm, src_hbm, so_hbm, si_hbm, st_hbm, phi_hbm, inv_hbm,
    res, modal,
    adj, jac, vol, src, so, si, st, phi, inv,
    inbox, outbox, mixed, halo_out, halo_in, gmat, row_out, row_in,
    local_sem, jac_sem, a_send, a_recv, b_send, b_recv, h_send, h_recv, m_send, m_recv,
):
    me = lax.axis_index("inst")
    sp = lax.axis_index("space")
    core = lax.rem(me, 2)
    chip = lax.div(me, 2)
    nc = ni // 2
    nv, nx, ny, nz = adj.shape
    halves = ny // 8

    def spot(c):
        return lax.div(c, halves), pl.multiple_of(lax.rem(c, halves) * 8, 8)

    small = [(adj_hbm.at[0], adj), (st_hbm, st), (phi_hbm, phi), (so_hbm, so), (inv_hbm, inv),
             (si_hbm, si), (vol_hbm, vol), (src_hbm.at[0], src)]
    copies = [pltpu.make_async_copy(a, b, local_sem.at[n]) for n, (a, b) in enumerate(small)]
    edge1 = pltpu.make_async_copy(jac_hbm.at[0, 1, :, :, nx - 1], jac.at[1, :, :, nx - 1], jac_sem.at[7])
    edge2 = pltpu.make_async_copy(jac_hbm.at[0, 2, :, :, 0], jac.at[2, :, :, 0], jac_sem.at[8])
    rest1 = pltpu.make_async_copy(jac_hbm.at[0, 1, :, :, 0:nx - 1], jac.at[1, :, :, 0:nx - 1], jac_sem.at[1])
    rest2 = pltpu.make_async_copy(jac_hbm.at[0, 2, :, :, 1:nx], jac.at[2, :, :, 1:nx], jac_sem.at[2])
    bulk = [pltpu.make_async_copy(jac_hbm.at[0, d], jac.at[d], jac_sem.at[d]) for d in (0, 3, 4, 5, 6)]
    for c in copies[:4]:
        c.start()
    edge1.start()
    edge2.start()
    for c in copies[4:]:
        c.start()
    rest1.start()
    rest2.start()
    for c in bulk:
        c.start()

    barrier = pltpu.get_barrier_semaphore()
    for k in range(1, ni):
        pl.semaphore_signal(barrier, inc=1, device_id={"inst": lax.rem(me + k, ni)}, device_id_type=MESH)
    for k in range(1, ns):
        pl.semaphore_signal(barrier, inc=1, device_id={"space": lax.rem(sp + k, ns)}, device_id_type=MESH)

    copies[1].wait()
    copies[2].wait()
    hi = phi[...].astype(jnp.bfloat16)
    lo = (phi[...] - hi.astype(jnp.float32)).astype(jnp.bfloat16)
    stations = phi.shape[1]
    modes = phi.shape[0]
    row_id = lax.broadcasted_iota(jnp.int32, (stations, nz), 0)
    for x in range(nx):
        onehot = (row_id == st[x:x + 1, :]).astype(jnp.float32).astype(jnp.bfloat16)
        gmat[x] = (jnp.dot(hi, onehot, preferred_element_type=jnp.float32)
                   + jnp.dot(lo, onehot, preferred_element_type=jnp.float32))

    copies[0].wait()
    pl.semaphore_wait(barrier, ni - 1 + ns - 1)

    def to_mixer(dc, cc):
        other = lax.rem(chip + dc, nc)
        peer = other * 2 + cc
        x, y = spot(other)
        return pltpu.make_async_remote_copy(
            src_ref=adj.at[pl.ds(FIRST[cc], COUNT[cc]), x, pl.ds(y, 8), :],
            dst_ref=inbox.at[me, pl.ds(0, COUNT[cc])],
            send_sem=a_send.at[dc * 2 + cc], recv_sem=a_recv.at[me],
            device_id={"inst": peer}, device_id_type=MESH)

    def others(act):
        for dc in range(1, nc):
            for cc in range(2):
                act(dc, cc)
        for cc in range(2):
            @pl.when(core != cc)
            def _():
                act(0, cc)

    others(lambda dc, cc: to_mixer(dc, cc).start())

    def halo(side):
        step = 1 if side == 0 else ns - 1
        return pltpu.make_async_remote_copy(
            src_ref=halo_out.at[side], dst_ref=halo_in.at[side],
            send_sem=h_send.at[side], recv_sem=h_recv.at[side],
            device_id={"space": lax.rem(sp + step, ns)}, device_id_type=MESH)

    def product(d, j, x):
        total = jac[d, 0, j, x] * adj[0, x]
        for i in range(1, nv):
            total = total + jac[d, i, j, x] * adj[i, x]
        return total

    edge1.wait()
    edge2.wait()
    for side, d, x in ((0, 1, nx - 1), (1, 2, 0)):
        for j in range(nv):
            halo_out[side, j] = product(d, j, x)
        halo(side).start()

    copies[3].wait()
    col = jnp.zeros((modes, nz), jnp.float32)
    for x in range(nx):
        face = so[0, x:x + 1, :] * adj[0, x, 0:1, :]
        for j in range(1, nv):
            face = face + so[j, x:x + 1, :] * adj[j, x, 0:1, :]
        col = col + gmat[x] * face
    col = jnp.sum(col, axis=1, keepdims=True)
    diag = (lax.broadcasted_iota(jnp.int32, (modes, nz), 0)
            == lax.broadcasted_iota(jnp.int32, (modes, nz), 1))
    share = jnp.sum(jnp.where(diag, col, 0.0), axis=0, keepdims=True)
    row_out[...] = share
    row_in[sp] = share

    def to_block(k):
        return pltpu.make_async_remote_copy(
            src_ref=row_out, dst_ref=row_in.at[sp],
            send_sem=m_send.at[k], recv_sem=m_recv.at[sp],
            device_id={"space": lax.rem(sp + k, ns)}, device_id_type=MESH)

    for k in range(1, ns):
        to_block(k).start()

    rest1.wait()
    rest2.wait()
    for c in bulk:
        c.wait()
    copies[7].wait()
    row = lax.broadcasted_iota(jnp.int32, (ny, nz), 0)
    lane = lax.broadcasted_iota(jnp.int32, (ny, nz), 1)

    def flux(j, carry):
        for x in range(nx):
            total = product(0, j, x) - src[j, x]
            if x > 0:
                total = total + product(1, j, x - 1)
            if x < nx - 1:
                total = total + product(2, j, x + 1)
            total = total + jnp.where(row == 0, 0.0, pltpu.roll(product(3, j, x), 1, 0))
            total = total + jnp.where(row == ny - 1, 0.0, pltpu.roll(product(4, j, x), ny - 1, 0))
            total = total + jnp.where(lane == 0, 0.0, pltpu.roll(product(5, j, x), 1, 1))
            total = total + jnp.where(lane == nz - 1, 0.0, pltpu.roll(product(6, j, x), nz - 1, 1))
            res[j, x] = total
        return carry

    lax.fori_loop(0, nv, flux, 0)

    my_x, my_y = spot(chip)
    for cc in range(2):
        @pl.when(core == cc)
        def _():
            inbox[me, 0:COUNT[cc]] = adj[FIRST[cc]:FIRST[cc] + COUNT[cc], my_x, pl.ds(my_y, 8), :]

            def arrival(dc, oc):
                source = lax.rem(chip + dc, nc) * 2 + oc
                block = inbox.at[source, pl.ds(0, COUNT[cc])]
                return pltpu.make_async_remote_copy(
                    src_ref=block, dst_ref=block, send_sem=a_send.at[dc * 2 + oc], recv_sem=a_recv.at[source],
                    device_id={"inst": source}, device_id_type=MESH)

            others(lambda dc, oc: arrival(dc, oc).wait_recv())

    weight = time_weight(ni)
    half = ni // 2

    def mix(t, carry):
        a = [inbox[lax.rem(me + k, ni), t] for k in range(ni)]
        even = [a[k] + a[k + half] for k in range(half)]
        odd = [a[k] - a[k + half] for k in range(half)]
        for d in range(half):
            near = [float(weight[(k - d) % ni]) for k in range(half)]
            far = [float(weight[(k - d + half) % ni]) for k in range(half)]
            plus = sum(even[k] * np.float32(0.5 * (near[k] + far[k])) for k in range(half))
            minus = sum(odd[k] * np.float32(0.5 * (near[k] - far[k])) for k in range(half))
            outbox[lax.rem(me + d, ni), t] = plus + minus
            outbox[lax.rem(me + d + half, ni), t] = plus - minus
        return carry

    lax.fori_loop(0, 3 - core, mix, 0)

    def back_home(cc, dc, oc):
        peer = lax.rem(chip + dc, nc) * 2 + oc
        return pltpu.make_async_remote_copy(
            src_ref=outbox.at[peer, pl.ds(0, COUNT[cc])],
            dst_ref=mixed.at[pl.ds(FIRST[cc], COUNT[cc]), my_x, pl.ds(my_y, 8), :],
            send_sem=b_send.at[dc * 2 + oc], recv_sem=b_recv.at[me],
            device_id={"inst": peer}, device_id_type=MESH)

    for cc in range(2):
        @pl.when(core == cc)
        def _():
            others(lambda dc, oc: back_home(cc, dc, oc).start())
            mixed[FIRST[cc]:FIRST[cc] + COUNT[cc], my_x, pl.ds(my_y, 8), :] = outbox[me, 0:COUNT[cc]]

    def row_arrival(k):
        source = lax.rem(sp + k, ns)
        return pltpu.make_async_remote_copy(
            src_ref=row_out, dst_ref=row_in.at[source], send_sem=m_send.at[k], recv_sem=m_recv.at[source],
            device_id={"space": source}, device_id_type=MESH)

    for k in range(1, ns):
        row_arrival(k).wait_recv()
    copies[4].wait()
    copies[5].wait()
    copies[6].wait()
    sums = jnp.sum(row_in[...], axis=0)
    coords = sums[:, 0:modes] * inv[...]
    modal[...] = coords
    square = (lax.broadcasted_iota(jnp.int32, (modes, modes), 0)
              == lax.broadcasted_iota(jnp.int32, (modes, modes), 1))
    column = jnp.sum(jnp.where(square, coords, 0.0), axis=1, keepdims=True)
    for x in range(nx):
        back = jnp.sum(gmat[x] * column, axis=0, keepdims=True)
        for j in range(nv):
            res[j, x, 0:1, :] = res[j, x, 0:1, :] + si[j, x:x + 1, :] * back

    halo(0).wait_recv()
    halo(1).wait_recv()
    for j in range(nv):
        res[j, 0] = res[j, 0] + halo_in[0, j]
        res[j, nx - 1] = res[j, nx - 1] + halo_in[1, j]

    def home_arrival(dc, oc):
        other = lax.rem(chip + dc, nc)
        x, y = spot(other)
        block = mixed.at[pl.ds(FIRST[oc], COUNT[oc]), x, pl.ds(y, 8), :]
        return pltpu.make_async_remote_copy(
            src_ref=block, dst_ref=block, send_sem=b_send.at[dc * 2 + oc], recv_sem=b_recv.at[other * 2 + oc],
            device_id={"inst": other * 2 + oc}, device_id_type=MESH)

    others(lambda dc, oc: home_arrival(dc, oc).wait_recv())
    for j in range(nv):
        for x in range(nx):
            res[j, x] = res[j, x] + vol[x] * mixed[j, x]

    others(lambda dc, cc: to_mixer(dc, cc).wait_send())
    for cc in range(2):
        @pl.when(core == cc)
        def _():
            others(lambda dc, oc: back_home(cc, dc, oc).wait_send())
    halo(0).wait_send()
    halo(1).wait_send()
    for k in range(1, ns):
        to_block(k).wait_send()


def solution(mesh):
    ni, ns = mesh.shape["inst"], mesh.shape["space"]
    placed = (
        P("inst", None, "space", None, None),
        P("inst", None, None, None, "space", None, None),
        P("space", None, None),
        P("inst", None, "space", None, None),
        P(None, "space", None),
        P(None, "space", None),
        P("space", None),
        P(),
        P(),
    )

    def body(adjoint, jacobian, volume, source, surface_out, surface_in, station, phi, inv_stiff):
        _, nv, nx, ny, nz = adjoint.shape
        modes, stations = phi.shape
        inv_row = inv_stiff.reshape(1, modes)
        f32 = jnp.float32
        operands = (adjoint, jacobian, volume, source, surface_out, surface_in, station, phi, inv_row)
        vmem = pltpu.VMEM
        sem = pltpu.SemaphoreType.DMA
        residual, modal = pl.pallas_call(
            functools.partial(kernel, ni, ns),
            out_shape=(jax.ShapeDtypeStruct((nv, nx, ny, nz), f32), jax.ShapeDtypeStruct((1, modes), f32)),
            in_specs=[pl.BlockSpec(memory_space=pltpu.HBM)] * len(operands),
            out_specs=(pl.BlockSpec(memory_space=pltpu.VMEM), pl.BlockSpec(memory_space=pltpu.VMEM)),
            scratch_shapes=[
                vmem((nv, nx, ny, nz), f32), vmem(jacobian.shape[1:], f32), vmem((nx, ny, nz), f32),
                vmem((nv, nx, ny, nz), f32), vmem((nv, nx, nz), f32), vmem((nv, nx, nz), f32),
                vmem((nx, nz), jnp.int32), vmem((modes, stations), f32), vmem((1, modes), f32),
                vmem((ni, 3, 8, nz), f32), vmem((ni, 3, 8, nz), f32), vmem((nv, nx, ny, nz), f32),
                vmem((2, nv, ny, nz), f32), vmem((2, nv, ny, nz), f32), vmem((nx, modes, nz), f32),
                vmem((1, nz), f32), vmem((ns, 1, nz), f32),
                sem((8,)), sem((9,)), sem((ni,)), sem((ni,)), sem((ni,)), sem((ni,)),
                sem((2,)), sem((2,)), sem((ns,)), sem((ns,)),
            ],
            compiler_params=pltpu.CompilerParams(
                collective_id=0, has_side_effects=True, vmem_limit_bytes=24 << 20),
        )(*[pltpu.with_memory_space_constraint(x, pltpu.HBM) for x in operands])
        return residual[None], modal

    return jax.shard_map(
        body, mesh=mesh, in_specs=placed,
        out_specs=(P("inst", None, "space", None, None), P("inst", None)), check_vma=False)
```

time: 76.6 us -> 24.7 us (0.32)
  the two profiles are of different devices: /device:TPU:6 before, /device:TPU:1 now
where the time goes in v1:
time: 24.7 us; the launch traced here: 24.6 us
  Pallas kernels  22.8 us (92%)
  local copies, waits for them, and re-layouts  1.18 us (5%)
  between operations  0.64 us (3%)
    pallas_call x1, Pallas kernels, body(): pl.pallas_call(functools.partial(kernel, ni, ns), out_shape=(jax.ShapeDty...  22.8 us
    unnamed x2, local copies, waits for them, and re-layouts  1.18 us

profile of v1, /device:TPU:1, one launch (start us, length us, event | category | flops | bytes accessed | tf_op | source)
XLA Modules:
  0.0 24.6 jit_solution(667678204476188152)
XLA Ops:
  0.6 22.8 %shard_map.104 = (f32[5,4,16,128]{3,2,1,0:T(8,128)S(1)}, f32[1,40]{1,0:T(1,128)S(1)}) custom-call(f32[1,5,4,16,128]{4,3,2,1,0:T(8,128)} %adj_hbm.1, f32[1,7,5,5,4,16,128]{6,5,4,3,2,1,0:T(8,128)} %jac_hbm.1, f32[4,16,128]{2,1,0:T(8,128)} %vol_hbm.1, f32[1,5,4,16,128]{4,3,2,1,0:T(8,128)} %src_hbm.1, f32[5,4,128]{2,1,0:T(4,128)} %so_hbm.1, ...), custom_call_target="tpu_custom_call" | custom-call | tf_op jit(solution)/shard_map/pallas_call | solution.py:294
  23.4 0.7 %copy.13 = f32[1,5,4,16,128]{4,3,2,1,0:T(8,128)} copy(f32[1,5,4,16,128]{4,3,2,1,0:T(8,128)S(1)} %bitcast.2) | data formatting | bytes 327680
  24.1 0.5 %copy.14 = f32[1,40]{1,0:T(1,128)} copy(f32[1,40]{1,0:T(1,128)S(1)} %get-tuple-element.9) | data formatting | bytes 320

commit v2 on v1

--- a/solution.py
+++ b/solution.py
@@ -30,6 +30,7 @@
     adj, jac, vol, src, so, si, st, phi, inv,
     inbox, outbox, mixed, halo_out, halo_in, gmat, row_out, row_in,
     local_sem, jac_sem, a_send, a_recv, b_send, b_recv, h_send, h_recv, m_send, m_recv,
+    ready_inst, ready_space,
 ):
     me = lax.axis_index("inst")
     sp = lax.axis_index("space")
@@ -62,10 +63,15 @@
         c.start()
 
     barrier = pltpu.get_barrier_semaphore()
-    for k in range(1, ni):
-        pl.semaphore_signal(barrier, inc=1, device_id={"inst": lax.rem(me + k, ni)}, device_id_type=MESH)
-    for k in range(1, ns):
-        pl.semaphore_signal(barrier, inc=1, device_id={"space": lax.rem(sp + k, ns)}, device_id_type=MESH)
+
+
+    def signal_range(semaphore, axis, start, end):
+        @pl.loop(start, end)
+        def _(peer):
+            pl.semaphore_signal(semaphore, inc=1, device_id={axis: peer}, device_id_type=MESH)
+
+    signal_range(barrier, "space", sp + 1, ns)
+    signal_range(barrier, "inst", me + 1, ni)
 
     copies[1].wait()
     copies[2].wait()
@@ -80,49 +86,6 @@
                    + jnp.dot(lo, onehot, preferred_element_type=jnp.float32))
 
     copies[0].wait()
-    pl.semaphore_wait(barrier, ni - 1 + ns - 1)
-
-    def to_mixer(dc, cc):
-        other = lax.rem(chip + dc, nc)
-        peer = other * 2 + cc
-        x, y = spot(other)
-        return pltpu.make_async_remote_copy(
-            src_ref=adj.at[pl.ds(FIRST[cc], COUNT[cc]), x, pl.ds(y, 8), :],
-            dst_ref=inbox.at[me, pl.ds(0, COUNT[cc])],
-            send_sem=a_send.at[dc * 2 + cc], recv_sem=a_recv.at[me],
-            device_id={"inst": peer}, device_id_type=MESH)
-
-    def others(act):
-        for dc in range(1, nc):
-            for cc in range(2):
-                act(dc, cc)
-        for cc in range(2):
-            @pl.when(core != cc)
-            def _():
-                act(0, cc)
-
-    others(lambda dc, cc: to_mixer(dc, cc).start())
-
-    def halo(side):
-        step = 1 if side == 0 else ns - 1
-        return pltpu.make_async_remote_copy(
-            src_ref=halo_out.at[side], dst_ref=halo_in.at[side],
-            send_sem=h_send.at[side], recv_sem=h_recv.at[side],
-            device_id={"space": lax.rem(sp + step, ns)}, device_id_type=MESH)
-
-    def product(d, j, x):
-        total = jac[d, 0, j, x] * adj[0, x]
-        for i in range(1, nv):
-            total = total + jac[d, i, j, x] * adj[i, x]
-        return total
-
-    edge1.wait()
-    edge2.wait()
-    for side, d, x in ((0, 1, nx - 1), (1, 2, 0)):
-        for j in range(nv):
-            halo_out[side, j] = product(d, j, x)
-        halo(side).start()
-
     copies[3].wait()
     col = jnp.zeros((modes, nz), jnp.float32)
     for x in range(nx):
@@ -137,14 +100,88 @@
     row_out[...] = share
     row_in[sp] = share
 
-    def to_block(k):
+    def to_block(peer):
         return pltpu.make_async_remote_copy(
             src_ref=row_out, dst_ref=row_in.at[sp],
-            send_sem=m_send.at[k], recv_sem=m_recv.at[sp],
-            device_id={"space": lax.rem(sp + k, ns)}, device_id_type=MESH)
-
-    for k in range(1, ns):
-        to_block(k).start()
+            send_sem=m_send.at[peer], recv_sem=m_recv.at[sp],
+            device_id={"space": peer}, device_id_type=MESH)
+
+    @pl.when(me + sp > 0)
+    def _():
+        pl.semaphore_wait(barrier, me + sp)
+
+    @pl.loop(0, sp)
+    def _(peer):
+        to_block(peer).start()
+
+    signal_range(ready_inst, "inst", 0, me)
+    signal_range(ready_space, "space", 0, sp)
+
+    def to_mixer(other, cc):
+        x, y = spot(other)
+        return pltpu.make_async_remote_copy(
+            src_ref=adj.at[pl.ds(FIRST[cc], COUNT[cc]), x, pl.ds(y, 8), :],
+            dst_ref=inbox.at[me, pl.ds(0, COUNT[cc])],
+            send_sem=a_send.at[other * 2 + cc], recv_sem=a_recv.at[me],
+            device_id={"inst": other * 2 + cc}, device_id_type=MESH)
+
+    def before(act):
+        @pl.when(core == 1)
+        def _():
+            act(chip, 0)
+
+        @pl.loop(1, chip + 1)
+        def _(dc):
+            act(chip - dc, 0)
+            act(chip - dc, 1)
+
+    def after(act):
+        @pl.when(core == 0)
+        def _():
+            act(chip, 1)
+
+        @pl.loop(1, nc - chip)
+        def _(dc):
+            act(chip + dc, 0)
+            act(chip + dc, 1)
+
+    def others(act):
+        before(act)
+        after(act)
+
+    before(lambda c, cc: to_mixer(c, cc).start())
+
+    def halo(side):
+        step = 1 if side == 0 else ns - 1
+        return pltpu.make_async_remote_copy(
+            src_ref=halo_out.at[side], dst_ref=halo_in.at[side],
+            send_sem=h_send.at[side], recv_sem=h_recv.at[side],
+            device_id={"space": lax.rem(sp + step, ns)}, device_id_type=MESH)
+
+    def product(d, j, x):
+        total = jac[d, 0, j, x] * adj[0, x]
+        for i in range(1, nv):
+            total = total + jac[d, i, j, x] * adj[i, x]
+        return total
+
+    edge1.wait()
+    edge2.wait()
+    for side, d, x in ((0, 1, nx - 1), (1, 2, 0)):
+        for j in range(nv):
+            halo_out[side, j] = product(d, j, x)
+
+    @pl.when(sp == ns - 1)
+    def _():
+        halo(0).start()
+
+    @pl.when(sp > 0)
+    def _():
+        halo(1).start()
+
+    @pl.when(me < ni - 1)
+    def _():
+        pl.semaphore_wait(ready_inst, ni - 1 - me)
+    after(lambda c, cc: to_mixer(c, cc).start())
 
     rest1.wait()
     rest2.wait()
@@ -176,14 +213,14 @@
         def _():
             inbox[me, 0:COUNT[cc]] = adj[FIRST[cc]:FIRST[cc] + COUNT[cc], my_x, pl.ds(my_y, 8), :]
 
-            def arrival(dc, oc):
-                source = lax.rem(chip + dc, nc) * 2 + oc
+            def arrival(other, oc):
+                source = other * 2 + oc
                 block = inbox.at[source, pl.ds(0, COUNT[cc])]
                 return pltpu.make_async_remote_copy(
-                    src_ref=block, dst_ref=block, send_sem=a_send.at[dc * 2 + oc], recv_sem=a_recv.at[source],
+                    src_ref=block, dst_ref=block, send_sem=a_send.at[source], recv_sem=a_recv.at[source],
                     device_id={"inst": source}, device_id_type=MESH)
 
-            others(lambda dc, oc: arrival(dc, oc).wait_recv())
+            others(lambda c, oc: arrival(c, oc).wait_recv())
 
     weight = time_weight(ni)
     half = ni // 2
@@ -203,31 +240,73 @@
 
     lax.fori_loop(0, 3 - core, mix, 0)
 
-    def back_home(cc, dc, oc):
-        peer = lax.rem(chip + dc, nc) * 2 + oc
+    def back_home(cc, other, oc):
+        peer = other * 2 + oc
         return pltpu.make_async_remote_copy(
             src_ref=outbox.at[peer, pl.ds(0, COUNT[cc])],
             dst_ref=mixed.at[pl.ds(FIRST[cc], COUNT[cc]), my_x, pl.ds(my_y, 8), :],
-            send_sem=b_send.at[dc * 2 + oc], recv_sem=b_recv.at[me],
+            send_sem=b_send.at[peer], recv_sem=b_recv.at[me],
             device_id={"inst": peer}, device_id_type=MESH)
 
     for cc in range(2):
         @pl.when(core == cc)
         def _():
-            others(lambda dc, oc: back_home(cc, dc, oc).start())
+            others(lambda c, oc: back_home(cc, c, oc).start())
             mixed[FIRST[cc]:FIRST[cc] + COUNT[cc], my_x, pl.ds(my_y, 8), :] = outbox[me, 0:COUNT[cc]]
 
-    def row_arrival(k):
-        source = lax.rem(sp + k, ns)
-        return pltpu.make_async_remote_copy(
-            src_ref=row_out, dst_ref=row_in.at[source], send_sem=m_send.at[k], recv_sem=m_recv.at[source],
-            device_id={"space": source}, device_id_type=MESH)
-
-    for k in range(1, ns):
-        row_arrival(k).wait_recv()
+    @pl.when(sp < ns - 1)
+    def _():
+        pl.semaphore_wait(ready_space, ns - 1 - sp)
+
+    @pl.loop(sp + 1, ns)
+    def _(peer):
+        to_block(peer).start()
+
+    @pl.when(sp < ns - 1)
+    def _():
+        halo(0).start()
+
+    @pl.when(sp == 0)
+    def _():
+        halo(1).start()
+
+    def home_arrival(other, oc):
+        x, y = spot(other)
+        source = other * 2 + oc
+        block = mixed.at[pl.ds(FIRST[oc], COUNT[oc]), x, pl.ds(y, 8), :]
+        return pltpu.make_async_remote_copy(
+            src_ref=block, dst_ref=block, send_sem=b_send.at[source], recv_sem=b_recv.at[source],
+            device_id={"inst": source}, device_id_type=MESH)
+
     copies[4].wait()
     copies[5].wait()
     copies[6].wait()
+    others(lambda c, oc: home_arrival(c, oc).wait_recv())
+    for j in range(nv):
+        for x in range(nx):
+            res[j, x] = res[j, x] + vol[x] * mixed[j, x]
+
+    halo(0).wait_recv()
+    halo(1).wait_recv()
+    for j in range(nv):
+        res[j, 0] = res[j, 0] + halo_in[0, j]
+        res[j, nx - 1] = res[j, nx - 1] + halo_in[1, j]
+
+    def each_block(act):
+        @pl.loop(0, sp)
+        def _(peer):
+            act(peer)
+
+        @pl.loop(sp + 1, ns)
+        def _(peer):
+            act(peer)
+
+    def row_arrival(source):
+        return pltpu.make_async_remote_copy(
+            src_ref=row_out, dst_ref=row_in.at[source], send_sem=m_send.at[source], recv_sem=m_recv.at[source],
+            device_id={"space": source}, device_id_type=MESH)
+
+    each_block(lambda peer: row_arrival(peer).wait_recv())
     sums = jnp.sum(row_in[...], axis=0)
     coords = sums[:, 0:modes] * inv[...]
     modal[...] = coords
@@ -239,34 +318,14 @@
         for j in range(nv):
             res[j, x, 0:1, :] = res[j, x, 0:1, :] + si[j, x:x + 1, :] * back
 
-    halo(0).wait_recv()
-    halo(1).wait_recv()
-    for j in range(nv):
-        res[j, 0] = res[j, 0] + halo_in[0, j]
-        res[j, nx - 1] = res[j, nx - 1] + halo_in[1, j]
-
-    def home_arrival(dc, oc):
-        other = lax.rem(chip + dc, nc)
-        x, y = spot(other)
-        block = mixed.at[pl.ds(FIRST[oc], COUNT[oc]), x, pl.ds(y, 8), :]
-        return pltpu.make_async_remote_copy(
-            src_ref=block, dst_ref=block, send_sem=b_send.at[dc * 2 + oc], recv_sem=b_recv.at[other * 2 + oc],
-            device_id={"inst": other * 2 + oc}, device_id_type=MESH)
-
-    others(lambda dc, oc: home_arrival(dc, oc).wait_recv())
-    for j in range(nv):
-        for x in range(nx):
-            res[j, x] = res[j, x] + vol[x] * mixed[j, x]
-
-    others(lambda dc, cc: to_mixer(dc, cc).wait_send())
+    others(lambda c, cc: to_mixer(c, cc).wait_send())
     for cc in range(2):
         @pl.when(core == cc)
         def _():
-            others(lambda dc, oc: back_home(cc, dc, oc).wait_send())
+            others(lambda c, oc: back_home(cc, c, oc).wait_send())
     halo(0).wait_send()
     halo(1).wait_send()
-    for k in range(1, ns):
-        to_block(k).wait_send()
+    each_block(lambda peer: to_block(peer).wait_send())
 
 
 def solution(mesh):
@@ -305,6 +364,7 @@
                 vmem((1, nz), f32), vmem((ns, 1, nz), f32),
                 sem((8,)), sem((9,)), sem((ni,)), sem((ni,)), sem((ni,)), sem((ni,)),
                 sem((2,)), sem((2,)), sem((ns,)), sem((ns,)),
+                pltpu.SemaphoreType.REGULAR, pltpu.SemaphoreType.REGULAR,
             ],
             compiler_params=pltpu.CompilerParams(
                 collective_id=0, has_side_effects=True, vmem_limit_bytes=24 << 20),

time: 24.7 us -> 21.4 us (0.87)
  the two profiles are of different devices: /device:TPU:1 before, /device:TPU:225 now
where the time goes in v2:
time: 21.4 us; the launch traced here: 21.3 us
  Pallas kernels  19.5 us (91%)
  local copies, waits for them, and re-layouts  1.18 us (6%)
  between operations  0.64 us (3%)
    pallas_call x1, Pallas kernels, body(): pl.pallas_call(functools.partial(kernel, ni, ns), out_shape=(jax.ShapeDty...  19.5 us
    unnamed x2, local copies, waits for them, and re-layouts  1.18 us

profile of v2, /device:TPU:225, one launch (start us, length us, event | category | flops | bytes accessed | tf_op | source)
XLA Modules:
  0.0 21.3 jit_solution(16061381335412514011)
XLA Ops:
  0.6 19.5 %shard_map.104 = (f32[5,4,16,128]{3,2,1,0:T(8,128)S(1)}, f32[1,40]{1,0:T(1,128)S(1)}) custom-call(f32[1,5,4,16,128]{4,3,2,1,0:T(8,128)} %adj_hbm.1, f32[1,7,5,5,4,16,128]{6,5,4,3,2,1,0:T(8,128)} %jac_hbm.1, f32[4,16,128]{2,1,0:T(8,128)} %vol_hbm.1, f32[1,5,4,16,128]{4,3,2,1,0:T(8,128)} %src_hbm.1, f32[5,4,128]{2,1,0:T(4,128)} %so_hbm.1, ...), custom_call_target="tpu_custom_call" | custom-call | tf_op jit(solution)/shard_map/pallas_call | solution.py:353
  20.1 0.7 %copy.13 = f32[1,5,4,16,128]{4,3,2,1,0:T(8,128)} copy(f32[1,5,4,16,128]{4,3,2,1,0:T(8,128)S(1)} %bitcast.2) | data formatting | bytes 327680
  20.8 0.5 %copy.14 = f32[1,40]{1,0:T(1,128)} copy(f32[1,40]{1,0:T(1,128)S(1)} %get-tuple-element.9) | data formatting | bytes 320

commit v3 on v2

--- a/solution.py
+++ b/solution.py
@@ -73,17 +73,58 @@
     signal_range(barrier, "space", sp + 1, ns)
     signal_range(barrier, "inst", me + 1, ni)
 
+    @pl.when(me + sp > 0)
+    def _():
+        pl.semaphore_wait(barrier, me + sp)
+
+    signal_range(ready_inst, "inst", 0, me)
+    signal_range(ready_space, "space", 0, sp)
+
+    def to_mixer(other, cc):
+        x, y = spot(other)
+        return pltpu.make_async_remote_copy(
+            src_ref=adj_hbm.at[0, pl.ds(FIRST[cc], COUNT[cc]), x, pl.ds(y, 8), :],
+            dst_ref=inbox.at[me, pl.ds(0, COUNT[cc])],
+            send_sem=a_send.at[other * 2 + cc], recv_sem=a_recv.at[me],
+            device_id={"inst": other * 2 + cc}, device_id_type=MESH)
+
+    def before(act):
+        @pl.when(core == 1)
+        def _():
+            act(chip, 0)
+
+        @pl.loop(1, chip + 1)
+        def _(dc):
+            act(chip - dc, 0)
+            act(chip - dc, 1)
+
+    def after(act):
+        @pl.when(core == 0)
+        def _():
+            act(chip, 1)
+
+        @pl.loop(1, nc - chip)
+        def _(dc):
+            act(chip + dc, 0)
+            act(chip + dc, 1)
+
+    def others(act):
+        before(act)
+        after(act)
+
+    before(lambda c, cc: to_mixer(c, cc).start())
+
     copies[1].wait()
     copies[2].wait()
-    hi = phi[...].astype(jnp.bfloat16)
-    lo = (phi[...] - hi.astype(jnp.float32)).astype(jnp.bfloat16)
     stations = phi.shape[1]
     modes = phi.shape[0]
+    hi = phi[...].astype(jnp.bfloat16).astype(jnp.float32)
+    parts = jnp.concatenate([hi, phi[...] - hi], axis=0).astype(jnp.bfloat16)
     row_id = lax.broadcasted_iota(jnp.int32, (stations, nz), 0)
     for x in range(nx):
         onehot = (row_id == st[x:x + 1, :]).astype(jnp.float32).astype(jnp.bfloat16)
-        gmat[x] = (jnp.dot(hi, onehot, preferred_element_type=jnp.float32)
-                   + jnp.dot(lo, onehot, preferred_element_type=jnp.float32))
+        both = jnp.dot(parts, onehot, preferred_element_type=jnp.float32)
+        gmat[x] = both[:modes] + both[modes:]
 
     copies[0].wait()
     copies[3].wait()
@@ -106,50 +147,14 @@
             send_sem=m_send.at[peer], recv_sem=m_recv.at[sp],
             device_id={"space": peer}, device_id_type=MESH)
 
-    @pl.when(me + sp > 0)
-    def _():
-        pl.semaphore_wait(barrier, me + sp)
-
     @pl.loop(0, sp)
     def _(peer):
         to_block(peer).start()
 
-    signal_range(ready_inst, "inst", 0, me)
-    signal_range(ready_space, "space", 0, sp)
-
-    def to_mixer(other, cc):
-        x, y = spot(other)
-        return pltpu.make_async_remote_copy(
-            src_ref=adj.at[pl.ds(FIRST[cc], COUNT[cc]), x, pl.ds(y, 8), :],
-            dst_ref=inbox.at[me, pl.ds(0, COUNT[cc])],
-            send_sem=a_send.at[other * 2 + cc], recv_sem=a_recv.at[me],
-            device_id={"inst": other * 2 + cc}, device_id_type=MESH)
-
-    def before(act):
-        @pl.when(core == 1)
-        def _():
-            act(chip, 0)
-
-        @pl.loop(1, chip + 1)
-        def _(dc):
-            act(chip - dc, 0)
-            act(chip - dc, 1)
-
-    def after(act):
-        @pl.when(core == 0)
-        def _():
-            act(chip, 1)
-
-        @pl.loop(1, nc - chip)
-        def _(dc):
-            act(chip + dc, 0)
-            act(chip + dc, 1)
-
-    def others(act):
-        before(act)
-        after(act)
-
-    before(lambda c, cc: to_mixer(c, cc).start())
+    @pl.when(me < ni - 1)
+    def _():
+        pl.semaphore_wait(ready_inst, ni - 1 - me)
+    after(lambda c, cc: to_mixer(c, cc).start())
 
     def halo(side):
         step = 1 if side == 0 else ns - 1
@@ -177,11 +182,6 @@
     @pl.when(sp > 0)
     def _():
         halo(1).start()
-
-    @pl.when(me < ni - 1)
-    def _():
-        pl.semaphore_wait(ready_inst, ni - 1 - me)
-    after(lambda c, cc: to_mixer(c, cc).start())
 
     rest1.wait()
     rest2.wait()
@@ -326,6 +326,15 @@
     halo(0).wait_send()
     halo(1).wait_send()
     each_block(lambda peer: to_block(peer).wait_send())
+
+
+def put_out(res, modal, res_hbm, modal_hbm, sem):
+    first = pltpu.make_async_copy(res, res_hbm.at[0], sem.at[0])
+    second = pltpu.make_async_copy(modal, modal_hbm, sem.at[1])
+    first.start()
+    second.start()
+    first.wait()
+    second.wait()
 
 
 def solution(mesh):
@@ -369,7 +378,13 @@
             compiler_params=pltpu.CompilerParams(
                 collective_id=0, has_side_effects=True, vmem_limit_bytes=24 << 20),
         )(*[pltpu.with_memory_space_constraint(x, pltpu.HBM) for x in operands])
-        return residual[None], modal
+        return pl.pallas_call(
+            put_out,
+            out_shape=(jax.ShapeDtypeStruct((1, nv, nx, ny, nz), f32), jax.ShapeDtypeStruct((1, modes), f32)),
+            in_specs=[pl.BlockSpec(memory_space=vmem)] * 2,
+            out_specs=(pl.BlockSpec(memory_space=pltpu.HBM), pl.BlockSpec(memory_space=pltpu.HBM)),
+            scratch_shapes=[sem((2,))],
+        )(*[pltpu.with_memory_space_constraint(x, vmem) for x in (residual, modal)])
 
     return jax.shard_map(
         body, mesh=mesh, in_specs=placed,

time: 21.4 us -> 21.1 us (0.986)
  the two profiles are of different devices: /device:TPU:225 before, /device:TPU:1 now
where the time goes in v3:
time: 21.1 us; the launch traced here: 20.8 us
  Pallas kernels  20.2 us (96%)
  between operations  0.64 us (3%)
    pallas_call x1, Pallas kernels, body(): pl.pallas_call(functools.partial(kernel, ni, ns), out_shape=(jax.ShapeDty...  19.5 us
    pallas_call x1, Pallas kernels, body(): pl.pallas_call(put_out, out_shape=(jax.ShapeDtypeStruct((1, nv, nx, ny, n...  0.69 us

profile of v3, /device:TPU:1, one launch (start us, length us, event | category | flops | bytes accessed | tf_op | source)
XLA Modules:
  0.0 20.8 jit_solution(10137969861588979389)
XLA Ops:
  0.6 19.5 %shard_map.104 = (f32[5,4,16,128]{3,2,1,0:T(8,128)S(1)}, f32[1,40]{1,0:T(1,128)S(1)}) custom-call(f32[1,5,4,16,128]{4,3,2,1,0:T(8,128)} %adj_hbm.1, f32[1,7,5,5,4,16,128]{6,5,4,3,2,1,0:T(8,128)} %jac_hbm.1, f32[4,16,128]{2,1,0:T(8,128)} %vol_hbm.1, f32[1,5,4,16,128]{4,3,2,1,0:T(8,128)} %src_hbm.1, f32[5,4,128]{2,1,0:T(4,128)} %so_hbm.1, ...), custom_call_target="tpu_custom_call" | custom-call | tf_op jit(solution)/shard_map/pallas_call | solution.py:362
  20.1 0.7 %shard_map.105 = (f32[1,5,4,16,128]{4,3,2,1,0:T(8,128)}, f32[1,40]{1,0:T(1,128)}) custom-call(f32[5,4,16,128]{3,2,1,0:T(8,128)S(1)} %get-tuple-element.4.res, f32[1,40]{1,0:T(1,128)S(1)} %get-tuple-element.5.modal), custom_call_target="tpu_custom_call" | custom-call | tf_op jit(solution)/shard_map/pallas_call | solution.py:381

commit v4 on v3

--- a/solution.py
+++ b/solution.py
@@ -23,6 +23,11 @@
     return first - 0.25 * second
 
 
+def turn(block):
+    z, y = lax.div(block, 2), lax.rem(block, 2)
+    return jnp.where(z < 4, 10 * z, 51 + z) + 16 * y
+
+
 def kernel(
     ni, ns,
     adj_hbm, jac_hbm, vol_hbm, src_hbm, so_hbm, si_hbm, st_hbm, phi_hbm, inv_hbm,
@@ -30,7 +35,7 @@
     adj, jac, vol, src, so, si, st, phi, inv,
     inbox, outbox, mixed, halo_out, halo_in, gmat, row_out, row_in,
     local_sem, jac_sem, a_send, a_recv, b_send, b_recv, h_send, h_recv, m_send, m_recv,
-    ready_inst, ready_space,
+    ready_space,
 ):
     me = lax.axis_index("inst")
     sp = lax.axis_index("space")
@@ -43,7 +48,35 @@
     def spot(c):
         return lax.div(c, halves), pl.multiple_of(lax.rem(c, halves) * 8, 8)
 
-    small = [(adj_hbm.at[0], adj), (st_hbm, st), (phi_hbm, phi), (so_hbm, so), (inv_hbm, inv),
+    def send_signals(semaphore, axis, peer):
+        pl.semaphore_signal(semaphore, inc=1, device_id={axis: peer}, device_id_type=MESH)
+
+    barrier = pltpu.get_barrier_semaphore()
+
+    @pl.loop(1, ni)
+    def _(k):
+        send_signals(barrier, "inst", lax.rem(me + k, ni))
+
+    my_turn = turn(sp)
+
+    def later_blocks(act):
+        @pl.loop(0, ns)
+        def _(peer):
+            @pl.when(turn(peer) > my_turn)
+            def _():
+                act(peer)
+
+    def earlier_blocks(act):
+        @pl.loop(0, ns)
+        def _(peer):
+            @pl.when(turn(peer) < my_turn)
+            def _():
+                act(peer)
+
+    later_blocks(lambda peer: send_signals(barrier, "space", peer))
+    n_earlier = sum(jnp.where(turn(jnp.int32(p)) < my_turn, 1, 0) for p in range(ns))
+
+    small = [(st_hbm, st), (phi_hbm, phi), (so_hbm, so), (adj_hbm.at[0], adj), (inv_hbm, inv),
              (si_hbm, si), (vol_hbm, vol), (src_hbm.at[0], src)]
     copies = [pltpu.make_async_copy(a, b, local_sem.at[n]) for n, (a, b) in enumerate(small)]
     edge1 = pltpu.make_async_copy(jac_hbm.at[0, 1, :, :, nx - 1], jac.at[1, :, :, nx - 1], jac_sem.at[7])
@@ -51,82 +84,22 @@
     rest1 = pltpu.make_async_copy(jac_hbm.at[0, 1, :, :, 0:nx - 1], jac.at[1, :, :, 0:nx - 1], jac_sem.at[1])
     rest2 = pltpu.make_async_copy(jac_hbm.at[0, 2, :, :, 1:nx], jac.at[2, :, :, 1:nx], jac_sem.at[2])
     bulk = [pltpu.make_async_copy(jac_hbm.at[0, d], jac.at[d], jac_sem.at[d]) for d in (0, 3, 4, 5, 6)]
-    for c in copies[:4]:
+    for c in copies[:4] + [edge1, edge2] + copies[4:] + [rest1, rest2] + bulk:
         c.start()
-    edge1.start()
-    edge2.start()
-    for c in copies[4:]:
-        c.start()
-    rest1.start()
-    rest2.start()
-    for c in bulk:
-        c.start()
-
-    barrier = pltpu.get_barrier_semaphore()
-
-
-    def signal_range(semaphore, axis, start, end):
-        @pl.loop(start, end)
-        def _(peer):
-            pl.semaphore_signal(semaphore, inc=1, device_id={axis: peer}, device_id_type=MESH)
-
-    signal_range(barrier, "space", sp + 1, ns)
-    signal_range(barrier, "inst", me + 1, ni)
-
-    @pl.when(me + sp > 0)
-    def _():
-        pl.semaphore_wait(barrier, me + sp)
-
-    signal_range(ready_inst, "inst", 0, me)
-    signal_range(ready_space, "space", 0, sp)
-
-    def to_mixer(other, cc):
-        x, y = spot(other)
-        return pltpu.make_async_remote_copy(
-            src_ref=adj_hbm.at[0, pl.ds(FIRST[cc], COUNT[cc]), x, pl.ds(y, 8), :],
-            dst_ref=inbox.at[me, pl.ds(0, COUNT[cc])],
-            send_sem=a_send.at[other * 2 + cc], recv_sem=a_recv.at[me],
-            device_id={"inst": other * 2 + cc}, device_id_type=MESH)
-
-    def before(act):
-        @pl.when(core == 1)
-        def _():
-            act(chip, 0)
-
-        @pl.loop(1, chip + 1)
-        def _(dc):
-            act(chip - dc, 0)
-            act(chip - dc, 1)
-
-    def after(act):
-        @pl.when(core == 0)
-        def _():
-            act(chip, 1)
-
-        @pl.loop(1, nc - chip)
-        def _(dc):
-            act(chip + dc, 0)
-            act(chip + dc, 1)
-
-    def others(act):
-        before(act)
-        after(act)
-
-    before(lambda c, cc: to_mixer(c, cc).start())
-
+
+    copies[0].wait()
     copies[1].wait()
+    modes, stations = phi.shape
+    for x in range(nx):
+        where = jnp.broadcast_to(st[x:x + 1, :], (modes, nz))
+        column = lax.rem(where, nz)
+        taken = jnp.zeros((modes, nz), jnp.float32)
+        for start in range(0, stations, nz):
+            found = jnp.take_along_axis(phi[:, start:start + nz], column, axis=1, mode="promise_in_bounds")
+            taken = jnp.where(where - column == start, found, taken)
+        gmat[x] = taken
+
     copies[2].wait()
-    stations = phi.shape[1]
-    modes = phi.shape[0]
-    hi = phi[...].astype(jnp.bfloat16).astype(jnp.float32)
-    parts = jnp.concatenate([hi, phi[...] - hi], axis=0).astype(jnp.bfloat16)
-    row_id = lax.broadcasted_iota(jnp.int32, (stations, nz), 0)
-    for x in range(nx):
-        onehot = (row_id == st[x:x + 1, :]).astype(jnp.float32).astype(jnp.bfloat16)
-        both = jnp.dot(parts, onehot, preferred_element_type=jnp.float32)
-        gmat[x] = both[:modes] + both[modes:]
-
-    copies[0].wait()
     copies[3].wait()
     col = jnp.zeros((modes, nz), jnp.float32)
     for x in range(nx):
@@ -141,28 +114,6 @@
     row_out[...] = share
     row_in[sp] = share
 
-    def to_block(peer):
-        return pltpu.make_async_remote_copy(
-            src_ref=row_out, dst_ref=row_in.at[sp],
-            send_sem=m_send.at[peer], recv_sem=m_recv.at[sp],
-            device_id={"space": peer}, device_id_type=MESH)
-
-    @pl.loop(0, sp)
-    def _(peer):
-        to_block(peer).start()
-
-    @pl.when(me < ni - 1)
-    def _():
-        pl.semaphore_wait(ready_inst, ni - 1 - me)
-    after(lambda c, cc: to_mixer(c, cc).start())
-
-    def halo(side):
-        step = 1 if side == 0 else ns - 1
-        return pltpu.make_async_remote_copy(
-            src_ref=halo_out.at[side], dst_ref=halo_in.at[side],
-            send_sem=h_send.at[side], recv_sem=h_recv.at[side],
-            device_id={"space": lax.rem(sp + step, ns)}, device_id_type=MESH)
-
     def product(d, j, x):
         total = jac[d, 0, j, x] * adj[0, x]
         for i in range(1, nv):
@@ -175,13 +126,55 @@
         for j in range(nv):
             halo_out[side, j] = product(d, j, x)
 
-    @pl.when(sp == ns - 1)
-    def _():
-        halo(0).start()
-
-    @pl.when(sp > 0)
-    def _():
-        halo(1).start()
+    pl.semaphore_wait(barrier, ni - 1 + n_earlier)
+
+    def to_block(peer):
+        return pltpu.make_async_remote_copy(
+            src_ref=row_out, dst_ref=row_in.at[sp],
+            send_sem=m_send.at[peer], recv_sem=m_recv.at[sp],
+            device_id={"space": peer}, device_id_type=MESH)
+
+    earlier_blocks(lambda peer: send_signals(ready_space, "space", peer))
+    earlier_blocks(lambda peer: to_block(peer).start())
+
+    def to_mixer(other, cc):
+        x, y = spot(other)
+        return pltpu.make_async_remote_copy(
+            src_ref=adj.at[pl.ds(FIRST[cc], COUNT[cc]), x, pl.ds(y, 8), :],
+            dst_ref=inbox.at[me, pl.ds(0, COUNT[cc])],
+            send_sem=a_send.at[other * 2 + cc], recv_sem=a_recv.at[me],
+            device_id={"inst": other * 2 + cc}, device_id_type=MESH)
+
+    def others(act):
+        @pl.loop(0, nc - 1)
+        def _(k):
+            chosen = lax.rem(chip + 1 + lax.rem(k + nc // 2 - 1, nc - 1), nc)
+            act(chosen, 0)
+            act(chosen, 1)
+
+        for cc in range(2):
+            @pl.when(core != cc)
+            def _():
+                act(chip, cc)
+
+    others(lambda c, cc: to_mixer(c, cc).start())
+
+    def halo(side):
+        peer = lax.rem(sp + (1 if side == 0 else ns - 1), ns)
+        return peer, pltpu.make_async_remote_copy(
+            src_ref=halo_out.at[side], dst_ref=halo_in.at[side],
+            send_sem=h_send.at[side], recv_sem=h_recv.at[side],
+            device_id={"space": peer}, device_id_type=MESH)
+
+    def send_halo(early):
+        for side in range(2):
+            peer, copy = halo(side)
+
+            @pl.when((turn(peer) < my_turn) if early else (turn(peer) > my_turn))
+            def _():
+                copy.start()
+
+    send_halo(True)
 
     rest1.wait()
     rest2.wait()
@@ -254,21 +247,12 @@
             others(lambda c, oc: back_home(cc, c, oc).start())
             mixed[FIRST[cc]:FIRST[cc] + COUNT[cc], my_x, pl.ds(my_y, 8), :] = outbox[me, 0:COUNT[cc]]
 
-    @pl.when(sp < ns - 1)
+    @pl.when(n_earlier < ns - 1)
     def _():
-        pl.semaphore_wait(ready_space, ns - 1 - sp)
-
-    @pl.loop(sp + 1, ns)
-    def _(peer):
-        to_block(peer).start()
-
-    @pl.when(sp < ns - 1)
-    def _():
-        halo(0).start()
-
-    @pl.when(sp == 0)
-    def _():
-        halo(1).start()
+        pl.semaphore_wait(ready_space, ns - 1 - n_earlier)
+
+    later_blocks(lambda peer: to_block(peer).start())
+    send_halo(False)
 
     def home_arrival(other, oc):
         x, y = spot(other)
@@ -286,8 +270,8 @@
         for x in range(nx):
             res[j, x] = res[j, x] + vol[x] * mixed[j, x]
 
-    halo(0).wait_recv()
-    halo(1).wait_recv()
+    halo(0)[1].wait_recv()
+    halo(1)[1].wait_recv()
     for j in range(nv):
         res[j, 0] = res[j, 0] + halo_in[0, j]
         res[j, nx - 1] = res[j, nx - 1] + halo_in[1, j]
@@ -323,8 +307,8 @@
         @pl.when(core == cc)
         def _():
             others(lambda c, oc: back_home(cc, c, oc).wait_send())
-    halo(0).wait_send()
-    halo(1).wait_send()
+    halo(0)[1].wait_send()
+    halo(1)[1].wait_send()
     each_block(lambda peer: to_block(peer).wait_send())
 
 
@@ -373,7 +357,7 @@
                 vmem((1, nz), f32), vmem((ns, 1, nz), f32),
                 sem((8,)), sem((9,)), sem((ni,)), sem((ni,)), sem((ni,)), sem((ni,)),
                 sem((2,)), sem((2,)), sem((ns,)), sem((ns,)),
-                pltpu.SemaphoreType.REGULAR, pltpu.SemaphoreType.REGULAR,
+                pltpu.SemaphoreType.REGULAR,
             ],
             compiler_params=pltpu.CompilerParams(
                 collective_id=0, has_side_effects=True, vmem_limit_bytes=24 << 20),

time: 21.1 us -> 19.8 us (0.938)
  the two profiles are of different devices: /device:TPU:1 before, /device:TPU:16 now
where the time goes in v4:
time: 19.8 us
  Pallas kernels  19.1 us (96%)
  between operations  0.64 us (3%)
    pallas_call x1, Pallas kernels, body(): pl.pallas_call(functools.partial(kernel, ni, ns), out_shape=(jax.ShapeDty...  18.4 us
    pallas_call x1, Pallas kernels, body(): pl.pallas_call(put_out, out_shape=(jax.ShapeDtypeStruct((1, nv, nx, ny, n...  0.69 us

profile of v4, /device:TPU:16, one launch (start us, length us, event | category | flops | bytes accessed | tf_op | source)
XLA Modules:
  0.0 19.8 jit_solution(18438847919031599095)
XLA Ops:
  0.6 18.4 %shard_map.104 = (f32[5,4,16,128]{3,2,1,0:T(8,128)S(1)}, f32[1,40]{1,0:T(1,128)S(1)}) custom-call(f32[1,5,4,16,128]{4,3,2,1,0:T(8,128)} %adj_hbm.1, f32[1,7,5,5,4,16,128]{6,5,4,3,2,1,0:T(8,128)} %jac_hbm.1, f32[4,16,128]{2,1,0:T(8,128)} %vol_hbm.1, f32[1,5,4,16,128]{4,3,2,1,0:T(8,128)} %src_hbm.1, f32[5,4,128]{2,1,0:T(4,128)} %so_hbm.1, ...), custom_call_target="tpu_custom_call" | custom-call | tf_op jit(solution)/shard_map/pallas_call | solution.py:346
  19.1 0.7 %shard_map.105 = (f32[1,5,4,16,128]{4,3,2,1,0:T(8,128)}, f32[1,40]{1,0:T(1,128)}) custom-call(f32[5,4,16,128]{3,2,1,0:T(8,128)S(1)} %get-tuple-element.4.res, f32[1,40]{1,0:T(1,128)S(1)} %get-tuple-element.5.modal), custom_call_target="tpu_custom_call" | custom-call | tf_op jit(solution)/shard_map/pallas_call | solution.py:365

commit v5 on v4

--- a/solution.py
+++ b/solution.py
@@ -61,7 +61,10 @@
 
     def later_blocks(act):
         @pl.loop(0, ns)
-        def _(peer):
+        def _(k):
+            far = k - ns // 2
+            peer = jnp.where(far < 0, k, ns // 2 + lax.rem(2 * far + ns, ns // 2) + lax.div(far, ns // 4))
+
             @pl.when(turn(peer) > my_turn)
             def _():
                 act(peer)
@@ -134,7 +137,7 @@
             send_sem=m_send.at[peer], recv_sem=m_recv.at[sp],
             device_id={"space": peer}, device_id_type=MESH)
 
-    earlier_blocks(lambda peer: send_signals(ready_space, "space", peer))
+    earlier_blocks(lambda peer: send_signals(ready_space.at[sp], "space", peer))
     earlier_blocks(lambda peer: to_block(peer).start())
 
     def to_mixer(other, cc):
@@ -166,15 +169,12 @@
             send_sem=h_send.at[side], recv_sem=h_recv.at[side],
             device_id={"space": peer}, device_id_type=MESH)
 
-    def send_halo(early):
-        for side in range(2):
-            peer, copy = halo(side)
-
-            @pl.when((turn(peer) < my_turn) if early else (turn(peer) > my_turn))
-            def _():
-                copy.start()
-
-    send_halo(True)
+    for side in range(2):
+        target, copy = halo(side)
+
+        @pl.when(turn(target) < my_turn)
+        def _():
+            copy.start()
 
     rest1.wait()
     rest2.wait()
@@ -200,6 +200,18 @@
 
     lax.fori_loop(0, nv, flux, 0)
 
+    def is_near(peer):
+        return jnp.where(jnp.where(peer > sp, peer - sp, sp - peer) == 1, 1, 0)
+
+    for side in range(2):
+        target, copy = halo(side)
+
+        @pl.when((turn(target) > my_turn) & (is_near(target) == 1))
+        def _():
+            pl.semaphore_wait(ready_space.at[target], 1)
+            copy.start()
+            to_block(target).start()
+
     my_x, my_y = spot(chip)
     for cc in range(2):
         @pl.when(core == cc)
@@ -247,12 +259,21 @@
             others(lambda c, oc: back_home(cc, c, oc).start())
             mixed[FIRST[cc]:FIRST[cc] + COUNT[cc], my_x, pl.ds(my_y, 8), :] = outbox[me, 0:COUNT[cc]]
 
-    @pl.when(n_earlier < ns - 1)
-    def _():
-        pl.semaphore_wait(ready_space, ns - 1 - n_earlier)
-
-    later_blocks(lambda peer: to_block(peer).start())
-    send_halo(False)
+    def late(peer):
+        @pl.when(is_near(peer) == 0)
+        def _():
+            pl.semaphore_wait(ready_space.at[peer], 1)
+            to_block(peer).start()
+
+    later_blocks(late)
+    for side in range(2):
+        target, copy = halo(side)
+
+        @pl.when((turn(target) > my_turn) & (is_near(target) == 0))
+        def _():
+            copy.start()
+
+    others(lambda c, cc: to_mixer(c, cc).wait_send())
 
     def home_arrival(other, oc):
         x, y = spot(other)
@@ -265,11 +286,6 @@
     copies[4].wait()
     copies[5].wait()
     copies[6].wait()
-    others(lambda c, oc: home_arrival(c, oc).wait_recv())
-    for j in range(nv):
-        for x in range(nx):
-            res[j, x] = res[j, x] + vol[x] * mixed[j, x]
-
     halo(0)[1].wait_recv()
     halo(1)[1].wait_recv()
     for j in range(nv):
@@ -302,14 +318,18 @@
         for j in range(nv):
             res[j, x, 0:1, :] = res[j, x, 0:1, :] + si[j, x:x + 1, :] * back
 
-    others(lambda c, cc: to_mixer(c, cc).wait_send())
-    for cc in range(2):
-        @pl.when(core == cc)
-        def _():
-            others(lambda c, oc: back_home(cc, c, oc).wait_send())
     halo(0)[1].wait_send()
     halo(1)[1].wait_send()
     each_block(lambda peer: to_block(peer).wait_send())
+    for cc in range(2):
+        @pl.when(core == cc)
+        def _():
+            others(lambda c, oc: back_home(cc, c, oc).wait_send())
+
+    others(lambda c, oc: home_arrival(c, oc).wait_recv())
+    for j in range(nv):
+        for x in range(nx):
+            res[j, x] = res[j, x] + vol[x] * mixed[j, x]
 
 
 def put_out(res, modal, res_hbm, modal_hbm, sem):
@@ -357,7 +377,7 @@
                 vmem((1, nz), f32), vmem((ns, 1, nz), f32),
                 sem((8,)), sem((9,)), sem((ni,)), sem((ni,)), sem((ni,)), sem((ni,)),
                 sem((2,)), sem((2,)), sem((ns,)), sem((ns,)),
-                pltpu.SemaphoreType.REGULAR,
+                pltpu.SemaphoreType.REGULAR((ns,)),
             ],
             compiler_params=pltpu.CompilerParams(
                 collective_id=0, has_side_effects=True, vmem_limit_bytes=24 << 20),

time: 19.8 us -> 19.3 us (0.975)
  the two profiles are of different devices: /device:TPU:16 before, /device:TPU:1 now
where the time goes in v5:
time: 19.3 us; the launch traced here: 19.2 us
  Pallas kernels  18.5 us (96%)
  between operations  0.64 us (3%)
    pallas_call x1, Pallas kernels, body(): pl.pallas_call(functools.partial(kernel, ni, ns), out_shape=(jax.ShapeDty...  17.8 us
    pallas_call x1, Pallas kernels, body(): pl.pallas_call(put_out, out_shape=(jax.ShapeDtypeStruct((1, nv, nx, ny, n...  0.69 us

profile of v5, /device:TPU:1, one launch (start us, length us, event | category | flops | bytes accessed | tf_op | source)
XLA Modules:
  0.0 19.2 jit_solution(10628155464825584651)
XLA Ops:
  0.6 17.8 %shard_map.104 = (f32[5,4,16,128]{3,2,1,0:T(8,128)S(1)}, f32[1,40]{1,0:T(1,128)S(1)}) custom-call(f32[1,5,4,16,128]{4,3,2,1,0:T(8,128)} %adj_hbm.1, f32[1,7,5,5,4,16,128]{6,5,4,3,2,1,0:T(8,128)} %jac_hbm.1, f32[4,16,128]{2,1,0:T(8,128)} %vol_hbm.1, f32[1,5,4,16,128]{4,3,2,1,0:T(8,128)} %src_hbm.1, f32[5,4,128]{2,1,0:T(4,128)} %so_hbm.1, ...), custom_call_target="tpu_custom_call" | custom-call | tf_op jit(solution)/shard_map/pallas_call | solution.py:366
  18.5 0.7 %shard_map.105 = (f32[1,5,4,16,128]{4,3,2,1,0:T(8,128)}, f32[1,40]{1,0:T(1,128)}) custom-call(f32[5,4,16,128]{3,2,1,0:T(8,128)S(1)} %get-tuple-element.4.res, f32[1,40]{1,0:T(1,128)S(1)} %get-tuple-element.5.modal), custom_call_target="tpu_custom_call" | custom-call | tf_op jit(solution)/shard_map/pallas_call | solution.py:385

commit v6 on v5

--- a/solution.py
+++ b/solution.py
@@ -21,6 +21,9 @@
     first = np.where(k != 0, 0.5 * parity * np.cos(angle) / safe, 0.0)
     second = np.where(k != 0, -0.5 * parity / (safe * safe), -(count * count + 2) / 12.0)
     return first - 0.25 * second
+
+
+SOON = 20
 
 
 def turn(block):
@@ -140,6 +143,20 @@
     earlier_blocks(lambda peer: send_signals(ready_space.at[sp], "space", peer))
     earlier_blocks(lambda peer: to_block(peer).start())
 
+    def halo(side):
+        peer = lax.rem(sp + (1 if side == 0 else ns - 1), ns)
+        return peer, pltpu.make_async_remote_copy(
+            src_ref=halo_out.at[side], dst_ref=halo_in.at[side],
+            send_sem=h_send.at[side], recv_sem=h_recv.at[side],
+            device_id={"space": peer}, device_id_type=MESH)
+
+    for side in range(2):
+        target, copy = halo(side)
+
+        @pl.when(turn(target) < my_turn)
+        def _():
+            copy.start()
+
     def to_mixer(other, cc):
         x, y = spot(other)
         return pltpu.make_async_remote_copy(
@@ -161,20 +178,6 @@
                 act(chip, cc)
 
     others(lambda c, cc: to_mixer(c, cc).start())
-
-    def halo(side):
-        peer = lax.rem(sp + (1 if side == 0 else ns - 1), ns)
-        return peer, pltpu.make_async_remote_copy(
-            src_ref=halo_out.at[side], dst_ref=halo_in.at[side],
-            send_sem=h_send.at[side], recv_sem=h_recv.at[side],
-            device_id={"space": peer}, device_id_type=MESH)
-
-    for side in range(2):
-        target, copy = halo(side)
-
-        @pl.when(turn(target) < my_turn)
-        def _():
-            copy.start()
 
     rest1.wait()
     rest2.wait()
@@ -200,17 +203,26 @@
 
     lax.fori_loop(0, nv, flux, 0)
 
-    def is_near(peer):
-        return jnp.where(jnp.where(peer > sp, peer - sp, sp - peer) == 1, 1, 0)
-
-    for side in range(2):
-        target, copy = halo(side)
-
-        @pl.when((turn(target) > my_turn) & (is_near(target) == 1))
-        def _():
-            pl.semaphore_wait(ready_space.at[target], 1)
-            copy.start()
-            to_block(target).start()
+    def is_soon(peer):
+        return turn(peer) - my_turn <= SOON
+
+    def to_later(soon):
+        def act(peer):
+            @pl.when(is_soon(peer) if soon else jnp.logical_not(is_soon(peer)))
+            def _():
+                pl.semaphore_wait(ready_space.at[peer], 1)
+                to_block(peer).start()
+
+        later_blocks(act)
+        for side in range(2):
+            target, copy = halo(side)
+            chosen = is_soon(target) if soon else jnp.logical_not(is_soon(target))
+
+            @pl.when((turn(target) > my_turn) & chosen)
+            def _():
+                copy.start()
+
+    to_later(True)
 
     my_x, my_y = spot(chip)
     for cc in range(2):
@@ -259,20 +271,7 @@
             others(lambda c, oc: back_home(cc, c, oc).start())
             mixed[FIRST[cc]:FIRST[cc] + COUNT[cc], my_x, pl.ds(my_y, 8), :] = outbox[me, 0:COUNT[cc]]
 
-    def late(peer):
-        @pl.when(is_near(peer) == 0)
-        def _():
-            pl.semaphore_wait(ready_space.at[peer], 1)
-            to_block(peer).start()
-
-    later_blocks(late)
-    for side in range(2):
-        target, copy = halo(side)
-
-        @pl.when((turn(target) > my_turn) & (is_near(target) == 0))
-        def _():
-            copy.start()
-
+    to_later(False)
     others(lambda c, cc: to_mixer(c, cc).wait_send())
 
     def home_arrival(other, oc):

time: 19.3 us -> 19.1 us (0.990)
  Pallas kernels: 18.5 us -> 18.3 us
    pallas_call x1, Pallas kernels: 17.8 us -> 17.7 us  [body(): pl.pallas_call(functools.partial(kernel, ni, ns), out_shape=(jax.ShapeDty...]
where the time goes in v6:
time: 19.1 us; the launch traced here: 19 us
  Pallas kernels  18.3 us (96%)
  between operations  0.64 us (3%)
    pallas_call x1, Pallas kernels, body(): pl.pallas_call(functools.partial(kernel, ni, ns), out_shape=(jax.ShapeDty...  17.7 us
    pallas_call x1, Pallas kernels, body(): pl.pallas_call(put_out, out_shape=(jax.ShapeDtypeStruct((1, nv, nx, ny, n...  0.69 us

profile of v6, /device:TPU:1, one launch (start us, length us, event | category | flops | bytes accessed | tf_op | source)
XLA Modules:
  0.0 19.0 jit_solution(11257707897767989043)
XLA Ops:
  0.6 17.7 %shard_map.104 = (f32[5,4,16,128]{3,2,1,0:T(8,128)S(1)}, f32[1,40]{1,0:T(1,128)S(1)}) custom-call(f32[1,5,4,16,128]{4,3,2,1,0:T(8,128)} %adj_hbm.1, f32[1,7,5,5,4,16,128]{6,5,4,3,2,1,0:T(8,128)} %jac_hbm.1, f32[4,16,128]{2,1,0:T(8,128)} %vol_hbm.1, f32[1,5,4,16,128]{4,3,2,1,0:T(8,128)} %src_hbm.1, f32[5,4,128]{2,1,0:T(4,128)} %so_hbm.1, ...), custom_call_target="tpu_custom_call" | custom-call | tf_op jit(solution)/shard_map/pallas_call | solution.py:365
  18.3 0.7 %shard_map.105 = (f32[1,5,4,16,128]{4,3,2,1,0:T(8,128)}, f32[1,40]{1,0:T(1,128)}) custom-call(f32[5,4,16,128]{3,2,1,0:T(8,128)S(1)} %get-tuple-element.4.res, f32[1,40]{1,0:T(1,128)S(1)} %get-tuple-element.5.modal), custom_call_target="tpu_custom_call" | custom-call | tf_op jit(solution)/shard_map/pallas_call | solution.py:384

commit v7 on v6

--- a/solution.py
+++ b/solution.py
@@ -24,6 +24,7 @@
 
 
 SOON = 20
+LATE = 40
 
 
 def turn(block):
@@ -36,7 +37,7 @@
     adj_hbm, jac_hbm, vol_hbm, src_hbm, so_hbm, si_hbm, st_hbm, phi_hbm, inv_hbm,
     res, modal,
     adj, jac, vol, src, so, si, st, phi, inv,
-    inbox, outbox, mixed, halo_out, halo_in, gmat, row_out, row_in,
+    inbox, outbox, mixed, gauge, halo_out, halo_in, gmat, row_out, row_in,
     local_sem, jac_sem, a_send, a_recv, b_send, b_recv, h_send, h_recv, m_send, m_recv,
     ready_space,
 ):
@@ -69,13 +70,6 @@
             peer = jnp.where(far < 0, k, ns // 2 + lax.rem(2 * far + ns, ns // 2) + lax.div(far, ns // 4))
 
             @pl.when(turn(peer) > my_turn)
-            def _():
-                act(peer)
-
-    def earlier_blocks(act):
-        @pl.loop(0, ns)
-        def _(peer):
-            @pl.when(turn(peer) < my_turn)
             def _():
                 act(peer)
 
@@ -137,11 +131,15 @@
     def to_block(peer):
         return pltpu.make_async_remote_copy(
             src_ref=row_out, dst_ref=row_in.at[sp],
-            send_sem=m_send.at[peer], recv_sem=m_recv.at[sp],
+            send_sem=m_send, recv_sem=m_recv,
             device_id={"space": peer}, device_id_type=MESH)
 
-    earlier_blocks(lambda peer: send_signals(ready_space.at[sp], "space", peer))
-    earlier_blocks(lambda peer: to_block(peer).start())
+    for peer in range(ns):
+        @pl.when(turn(jnp.int32(peer)) < my_turn)
+        def _():
+            to_block(peer).start()
+            send_signals(ready_space.at[sp], "space", peer)
+
 
     def halo(side):
         peer = lax.rem(sp + (1 if side == 0 else ns - 1), ns)
@@ -162,7 +160,7 @@
         return pltpu.make_async_remote_copy(
             src_ref=adj.at[pl.ds(FIRST[cc], COUNT[cc]), x, pl.ds(y, 8), :],
             dst_ref=inbox.at[me, pl.ds(0, COUNT[cc])],
-            send_sem=a_send.at[other * 2 + cc], recv_sem=a_recv.at[me],
+            send_sem=a_send, recv_sem=a_recv,
             device_id={"inst": other * 2 + cc}, device_id_type=MESH)
 
     def others(act):
@@ -224,20 +222,16 @@
 
     to_later(True)
 
+    def arrived(block, semaphore):
+        pltpu.make_async_copy(block, block, semaphore).wait()
+
     my_x, my_y = spot(chip)
     for cc in range(2):
         @pl.when(core == cc)
         def _():
             inbox[me, 0:COUNT[cc]] = adj[FIRST[cc]:FIRST[cc] + COUNT[cc], my_x, pl.ds(my_y, 8), :]
 
-            def arrival(other, oc):
-                source = other * 2 + oc
-                block = inbox.at[source, pl.ds(0, COUNT[cc])]
-                return pltpu.make_async_remote_copy(
-                    src_ref=block, dst_ref=block, send_sem=a_send.at[source], recv_sem=a_recv.at[source],
-                    device_id={"inst": source}, device_id_type=MESH)
-
-            others(lambda c, oc: arrival(c, oc).wait_recv())
+            arrived(inbox.at[pl.ds(0, ni - 1), pl.ds(0, COUNT[cc])], a_recv)
 
     weight = time_weight(ni)
     half = ni // 2
@@ -262,7 +256,7 @@
         return pltpu.make_async_remote_copy(
             src_ref=outbox.at[peer, pl.ds(0, COUNT[cc])],
             dst_ref=mixed.at[pl.ds(FIRST[cc], COUNT[cc]), my_x, pl.ds(my_y, 8), :],
-            send_sem=b_send.at[peer], recv_sem=b_recv.at[me],
+            send_sem=b_send, recv_sem=b_recv,
             device_id={"inst": peer}, device_id_type=MESH)
 
     for cc in range(2):
@@ -272,63 +266,64 @@
             mixed[FIRST[cc]:FIRST[cc] + COUNT[cc], my_x, pl.ds(my_y, 8), :] = outbox[me, 0:COUNT[cc]]
 
     to_later(False)
-    others(lambda c, cc: to_mixer(c, cc).wait_send())
-
-    def home_arrival(other, oc):
-        x, y = spot(other)
-        source = other * 2 + oc
-        block = mixed.at[pl.ds(FIRST[oc], COUNT[oc]), x, pl.ds(y, 8), :]
-        return pltpu.make_async_remote_copy(
-            src_ref=block, dst_ref=block, send_sem=b_send.at[source], recv_sem=b_recv.at[source],
-            device_id={"inst": source}, device_id_type=MESH)
-
+    for cc in range(2):
+        @pl.when(core == cc)
+        def _():
+            arrived(gauge.at[pl.ds(0, nv * nx * halves - COUNT[cc])], a_send)
+
+    arrived(row_in.at[pl.ds(0, ns - 1)], m_send)
     copies[4].wait()
     copies[5].wait()
     copies[6].wait()
-    halo(0)[1].wait_recv()
-    halo(1)[1].wait_recv()
-    for j in range(nv):
-        res[j, 0] = res[j, 0] + halo_in[0, j]
-        res[j, nx - 1] = res[j, nx - 1] + halo_in[1, j]
-
-    def each_block(act):
-        @pl.loop(0, sp)
-        def _(peer):
-            act(peer)
-
-        @pl.loop(sp + 1, ns)
-        def _(peer):
-            act(peer)
-
-    def row_arrival(source):
-        return pltpu.make_async_remote_copy(
-            src_ref=row_out, dst_ref=row_in.at[source], send_sem=m_send.at[source], recv_sem=m_recv.at[source],
-            device_id={"space": source}, device_id_type=MESH)
-
-    each_block(lambda peer: row_arrival(peer).wait_recv())
-    sums = jnp.sum(row_in[...], axis=0)
-    coords = sums[:, 0:modes] * inv[...]
-    modal[...] = coords
-    square = (lax.broadcasted_iota(jnp.int32, (modes, modes), 0)
-              == lax.broadcasted_iota(jnp.int32, (modes, modes), 1))
-    column = jnp.sum(jnp.where(square, coords, 0.0), axis=1, keepdims=True)
-    for x in range(nx):
-        back = jnp.sum(gmat[x] * column, axis=0, keepdims=True)
+
+    def add_mixed():
+        for cc in range(2):
+            @pl.when(core == cc)
+            def _():
+                arrived(gauge.at[pl.ds(0, nv * nx * halves - COUNT[cc])], b_recv)
+
         for j in range(nv):
-            res[j, x, 0:1, :] = res[j, x, 0:1, :] + si[j, x:x + 1, :] * back
+            for x in range(nx):
+                res[j, x] = res[j, x] + vol[x] * mixed[j, x]
+
+    def add_halo():
+        halo(0)[1].wait_recv()
+        halo(1)[1].wait_recv()
+        for j in range(nv):
+            res[j, 0] = res[j, 0] + halo_in[0, j]
+            res[j, nx - 1] = res[j, nx - 1] + halo_in[1, j]
+
+    def add_back():
+        arrived(row_in.at[pl.ds(0, ns - 1)], m_recv)
+        sums = jnp.sum(row_in[...], axis=0)
+        coords = sums[:, 0:modes] * inv[...]
+        modal[...] = coords
+        square = (lax.broadcasted_iota(jnp.int32, (modes, modes), 0)
+                  == lax.broadcasted_iota(jnp.int32, (modes, modes), 1))
+        column = jnp.sum(jnp.where(square, coords, 0.0), axis=1, keepdims=True)
+        for x in range(nx):
+            back = jnp.sum(gmat[x] * column, axis=0, keepdims=True)
+            for j in range(nv):
+                res[j, x, 0:1, :] = res[j, x, 0:1, :] + si[j, x:x + 1, :] * back
+
+    @pl.when(my_turn < LATE)
+    def _():
+        add_mixed()
+        add_halo()
+        add_back()
+
+    @pl.when(my_turn >= LATE)
+    def _():
+        add_back()
+        add_halo()
+        add_mixed()
 
     halo(0)[1].wait_send()
     halo(1)[1].wait_send()
-    each_block(lambda peer: to_block(peer).wait_send())
     for cc in range(2):
         @pl.when(core == cc)
         def _():
-            others(lambda c, oc: back_home(cc, c, oc).wait_send())
-
-    others(lambda c, oc: home_arrival(c, oc).wait_recv())
-    for j in range(nv):
-        for x in range(nx):
-            res[j, x] = res[j, x] + vol[x] * mixed[j, x]
+            arrived(inbox.at[pl.ds(0, ni - 1), pl.ds(0, COUNT[cc])], b_send)
 
 
 def put_out(res, modal, res_hbm, modal_hbm, sem):
@@ -372,10 +367,10 @@
                 vmem((nv, nx, ny, nz), f32), vmem((nv, nx, nz), f32), vmem((nv, nx, nz), f32),
                 vmem((nx, nz), jnp.int32), vmem((modes, stations), f32), vmem((1, modes), f32),
                 vmem((ni, 3, 8, nz), f32), vmem((ni, 3, 8, nz), f32), vmem((nv, nx, ny, nz), f32),
+                vmem((nv * nx * ny // 8, 8, nz), f32),
                 vmem((2, nv, ny, nz), f32), vmem((2, nv, ny, nz), f32), vmem((nx, modes, nz), f32),
                 vmem((1, nz), f32), vmem((ns, 1, nz), f32),
-                sem((8,)), sem((9,)), sem((ni,)), sem((ni,)), sem((ni,)), sem((ni,)),
-                sem((2,)), sem((2,)), sem((ns,)), sem((ns,)),
+                sem((8,)), sem((9,)), sem, sem, sem, sem, sem((2,)), sem((2,)), sem, sem,
                 pltpu.SemaphoreType.REGULAR((ns,)),
             ],
             compiler_params=pltpu.CompilerParams(

time: 19.1 us -> 17.8 us (0.932)
  Pallas kernels: 18.3 us -> 17.1 us
    pallas_call x1, Pallas kernels: 17.7 us -> 16.4 us  [body(): pl.pallas_call(functools.partial(kernel, ni, ns), out_shape=(jax.ShapeDty...]
where the time goes in v7:
time: 17.8 us; the launch traced here: 17.7 us
  Pallas kernels  17.1 us (96%)
  between operations  0.64 us (4%)
    pallas_call x1, Pallas kernels, body(): pl.pallas_call(functools.partial(kernel, ni, ns), out_shape=(jax.ShapeDty...  16.4 us
    pallas_call x1, Pallas kernels, body(): pl.pallas_call(put_out, out_shape=(jax.ShapeDtypeStruct((1, nv, nx, ny, n...  0.69 us

profile of v7, /device:TPU:1, one launch (start us, length us, event | category | flops | bytes accessed | tf_op | source)
XLA Modules:
  0.0 17.7 jit_solution(15745448516544763495)
XLA Ops:
  0.6 16.4 %shard_map.104 = (f32[5,4,16,128]{3,2,1,0:T(8,128)S(1)}, f32[1,40]{1,0:T(1,128)S(1)}) custom-call(f32[1,5,4,16,128]{4,3,2,1,0:T(8,128)} %adj_hbm.1, f32[1,7,5,5,4,16,128]{6,5,4,3,2,1,0:T(8,128)} %jac_hbm.1, f32[4,16,128]{2,1,0:T(8,128)} %vol_hbm.1, f32[1,5,4,16,128]{4,3,2,1,0:T(8,128)} %src_hbm.1, f32[5,4,128]{2,1,0:T(4,128)} %so_hbm.1, ...), custom_call_target="tpu_custom_call" | custom-call | tf_op jit(solution)/shard_map/pallas_call | solution.py:360
  17.0 0.7 %shard_map.105 = (f32[1,5,4,16,128]{4,3,2,1,0:T(8,128)}, f32[1,40]{1,0:T(1,128)}) custom-call(f32[5,4,16,128]{3,2,1,0:T(8,128)S(1)} %get-tuple-element.4.res, f32[1,40]{1,0:T(1,128)S(1)} %get-tuple-element.5.modal), custom_call_target="tpu_custom_call" | custom-call | tf_op jit(solution)/shard_map/pallas_call | solution.py:379

commit v8 on v7

--- a/solution.py
+++ b/solution.py
@@ -23,13 +23,17 @@
     return first - 0.25 * second
 
 
-SOON = 20
 LATE = 40
 
 
 def turn(block):
     z, y = lax.div(block, 2), lax.rem(block, 2)
     return jnp.where(z < 4, 10 * z, 51 + z) + 16 * y
+
+
+def turn_of(block):
+    z, y = divmod(block, 2)
+    return (10 * z if z < 4 else 51 + z) + 16 * y
 
 
 def kernel(
@@ -49,6 +53,8 @@
     nv, nx, ny, nz = adj.shape
     halves = ny // 8
 
+    far_first = sorted(range(1, nc), key=lambda k: abs(k - nc // 2))
+
     def spot(c):
         return lax.div(c, halves), pl.multiple_of(lax.rem(c, halves) * 8, 8)
 
@@ -57,24 +63,19 @@
 
     barrier = pltpu.get_barrier_semaphore()
 
-    @pl.loop(1, ni)
-    def _(k):
+    for k in sorted(range(1, ni), key=lambda k: abs(k - ni // 2)):
         send_signals(barrier, "inst", lax.rem(me + k, ni))
 
     my_turn = turn(sp)
 
     def later_blocks(act):
-        @pl.loop(0, ns)
-        def _(k):
-            far = k - ns // 2
-            peer = jnp.where(far < 0, k, ns // 2 + lax.rem(2 * far + ns, ns // 2) + lax.div(far, ns // 4))
-
-            @pl.when(turn(peer) > my_turn)
+        for peer in sorted(range(ns), key=turn_of):
+            @pl.when(turn_of(peer) > my_turn)
             def _():
                 act(peer)
 
     later_blocks(lambda peer: send_signals(barrier, "space", peer))
-    n_earlier = sum(jnp.where(turn(jnp.int32(p)) < my_turn, 1, 0) for p in range(ns))
+    n_earlier = sum(jnp.where(turn_of(p) < my_turn, 1, 0) for p in range(ns))
 
     small = [(st_hbm, st), (phi_hbm, phi), (so_hbm, so), (adj_hbm.at[0], adj), (inv_hbm, inv),
              (si_hbm, si), (vol_hbm, vol), (src_hbm.at[0], src)]
@@ -134,8 +135,8 @@
             send_sem=m_send, recv_sem=m_recv,
             device_id={"space": peer}, device_id_type=MESH)
 
-    for peer in range(ns):
-        @pl.when(turn(jnp.int32(peer)) < my_turn)
+    for peer in sorted(range(ns), key=turn_of):
+        @pl.when(turn_of(peer) < my_turn)
         def _():
             to_block(peer).start()
             send_signals(ready_space.at[sp], "space", peer)
@@ -164,9 +165,8 @@
             device_id={"inst": other * 2 + cc}, device_id_type=MESH)
 
     def others(act):
-        @pl.loop(0, nc - 1)
-        def _(k):
-            chosen = lax.rem(chip + 1 + lax.rem(k + nc // 2 - 1, nc - 1), nc)
+        for k in far_first:
+            chosen = lax.rem(chip + k, nc)
             act(chosen, 0)
             act(chosen, 1)
 
@@ -201,12 +201,12 @@
 
     lax.fori_loop(0, nv, flux, 0)
 
-    def is_soon(peer):
-        return turn(peer) - my_turn <= SOON
-
-    def to_later(soon):
+    def is_near(peer):
+        return jnp.where(peer > sp, peer - sp, sp - peer) == 1
+
+    def to_later(near):
         def act(peer):
-            @pl.when(is_soon(peer) if soon else jnp.logical_not(is_soon(peer)))
+            @pl.when(is_near(peer) if near else jnp.logical_not(is_near(peer)))
             def _():
                 pl.semaphore_wait(ready_space.at[peer], 1)
                 to_block(peer).start()
@@ -214,7 +214,7 @@
         later_blocks(act)
         for side in range(2):
             target, copy = halo(side)
-            chosen = is_soon(target) if soon else jnp.logical_not(is_soon(target))
+            chosen = is_near(target) if near else jnp.logical_not(is_near(target))
 
             @pl.when((turn(target) > my_turn) & chosen)
             def _():
@@ -236,34 +236,36 @@
     weight = time_weight(ni)
     half = ni // 2
 
-    def mix(t, carry):
-        a = [inbox[lax.rem(me + k, ni), t] for k in range(ni)]
-        even = [a[k] + a[k + half] for k in range(half)]
-        odd = [a[k] - a[k + half] for k in range(half)]
-        for d in range(half):
-            near = [float(weight[(k - d) % ni]) for k in range(half)]
-            far = [float(weight[(k - d + half) % ni]) for k in range(half)]
-            plus = sum(even[k] * np.float32(0.5 * (near[k] + far[k])) for k in range(half))
-            minus = sum(odd[k] * np.float32(0.5 * (near[k] - far[k])) for k in range(half))
-            outbox[lax.rem(me + d, ni), t] = plus + minus
-            outbox[lax.rem(me + d + half, ni), t] = plus - minus
-        return carry
-
-    lax.fori_loop(0, 3 - core, mix, 0)
-
-    def back_home(cc, other, oc):
-        peer = other * 2 + oc
+    def home(cc, d):
+        peer = lax.rem(me + d, ni)
         return pltpu.make_async_remote_copy(
             src_ref=outbox.at[peer, pl.ds(0, COUNT[cc])],
             dst_ref=mixed.at[pl.ds(FIRST[cc], COUNT[cc]), my_x, pl.ds(my_y, 8), :],
             send_sem=b_send, recv_sem=b_recv,
             device_id={"inst": peer}, device_id_type=MESH)
 
+    def mix(cc):
+        n = COUNT[cc]
+        a = [inbox[lax.rem(me + k, ni), 0:n] for k in range(ni)]
+        even = [a[k] + a[k + half] for k in range(half)]
+        odd = [a[k] - a[k + half] for k in range(half)]
+        for d in sorted(range(half), key=lambda d: d == 0):
+            near = [float(weight[(k - d) % ni]) for k in range(half)]
+            far = [float(weight[(k - d + half) % ni]) for k in range(half)]
+            plus = sum(even[k] * np.float32(0.5 * (near[k] + far[k])) for k in range(half))
+            minus = sum(odd[k] * np.float32(0.5 * (near[k] - far[k])) for k in range(half))
+            outbox[lax.rem(me + d + half, ni), 0:n] = plus - minus
+            home(cc, d + half).start()
+            if d:
+                outbox[lax.rem(me + d, ni), 0:n] = plus + minus
+                home(cc, d).start()
+            else:
+                mixed[FIRST[cc]:FIRST[cc] + n, my_x, pl.ds(my_y, 8), :] = plus + minus
+
     for cc in range(2):
         @pl.when(core == cc)
         def _():
-            others(lambda c, oc: back_home(cc, c, oc).start())
-            mixed[FIRST[cc]:FIRST[cc] + COUNT[cc], my_x, pl.ds(my_y, 8), :] = outbox[me, 0:COUNT[cc]]
+            mix(cc)
 
     to_later(False)
     for cc in range(2):

time: 17.8 us -> 17.9 us (level)
  no operation moved by 1% of the time
where the time goes in v8:
time: 17.9 us; the launch traced here: 17.8 us
  Pallas kernels  17.1 us (96%)
  between operations  0.64 us (4%)
    pallas_call x1, Pallas kernels, body(): pl.pallas_call(functools.partial(kernel, ni, ns), out_shape=(jax.ShapeDty...  16.5 us
    pallas_call x1, Pallas kernels, body(): pl.pallas_call(put_out, out_shape=(jax.ShapeDtypeStruct((1, nv, nx, ny, n...  0.69 us

profile of v8, /device:TPU:1, one launch (start us, length us, event | category | flops | bytes accessed | tf_op | source)
XLA Modules:
  0.0 17.8 jit_solution(12306872949386262468)
XLA Ops:
  0.6 16.5 %shard_map.104 = (f32[5,4,16,128]{3,2,1,0:T(8,128)S(1)}, f32[1,40]{1,0:T(1,128)S(1)}) custom-call(f32[1,5,4,16,128]{4,3,2,1,0:T(8,128)} %adj_hbm.1, f32[1,7,5,5,4,16,128]{6,5,4,3,2,1,0:T(8,128)} %jac_hbm.1, f32[4,16,128]{2,1,0:T(8,128)} %vol_hbm.1, f32[1,5,4,16,128]{4,3,2,1,0:T(8,128)} %src_hbm.1, f32[5,4,128]{2,1,0:T(4,128)} %so_hbm.1, ...), custom_call_target="tpu_custom_call" | custom-call | tf_op jit(solution)/shard_map/pallas_call | solution.py:362
  17.1 0.7 %shard_map.105 = (f32[1,5,4,16,128]{4,3,2,1,0:T(8,128)}, f32[1,40]{1,0:T(1,128)}) custom-call(f32[5,4,16,128]{3,2,1,0:T(8,128)S(1)} %get-tuple-element.4.res, f32[1,40]{1,0:T(1,128)S(1)} %get-tuple-element.5.modal), custom_call_target="tpu_custom_call" | custom-call | tf_op jit(solution)/shard_map/pallas_call | solution.py:381

commit v9 on v8

--- a/solution.py
+++ b/solution.py
@@ -24,6 +24,7 @@
 
 
 LATE = 40
+LEAN = 71
 
 
 def turn(block):
@@ -43,7 +44,7 @@
     adj, jac, vol, src, so, si, st, phi, inv,
     inbox, outbox, mixed, gauge, halo_out, halo_in, gmat, row_out, row_in,
     local_sem, jac_sem, a_send, a_recv, b_send, b_recv, h_send, h_recv, m_send, m_recv,
-    ready_space,
+    ready_space, relay,
 ):
     me = lax.axis_index("inst")
     sp = lax.axis_index("space")
@@ -53,7 +54,9 @@
     nv, nx, ny, nz = adj.shape
     halves = ny // 8
 
-    far_first = sorted(range(1, nc), key=lambda k: abs(k - nc // 2))
+    cx, cy, wide = lax.div(chip, 2), lax.rem(chip, 2), nc // 2
+    across = [lax.rem(cx + 2, wide) * 2 + y for y in range(2)]
+    beside = [lax.rem(cx + d, wide) * 2 + y for d in (1, wide - 1) for y in range(2)] + [cx * 2 + 1 - cy]
 
     def spot(c):
         return lax.div(c, halves), pl.multiple_of(lax.rem(c, halves) * 8, 8)
@@ -63,10 +66,19 @@
 
     barrier = pltpu.get_barrier_semaphore()
 
-    for k in sorted(range(1, ni), key=lambda k: abs(k - ni // 2)):
-        send_signals(barrier, "inst", lax.rem(me + k, ni))
-
     my_turn = turn(sp)
+    lean = my_turn >= LEAN
+
+    @pl.when(jnp.logical_not(lean))
+    def _():
+        for c in across:
+            for cc in range(2):
+                send_signals(barrier, "inst", c * 2 + cc)
+
+    for c in beside:
+        for cc in range(2):
+            send_signals(barrier, "inst", c * 2 + cc)
+    send_signals(barrier, "inst", chip * 2 + 1 - core)
 
     def later_blocks(act):
         for peer in sorted(range(ns), key=turn_of):
@@ -127,7 +139,11 @@
         for j in range(nv):
             halo_out[side, j] = product(d, j, x)
 
-    pl.semaphore_wait(barrier, ni - 1 + n_earlier)
+    pl.semaphore_wait(barrier, ni - 1 + n_earlier - jnp.where(lean, 2 * len(across), 0))
+
+    @pl.when(lean)
+    def _():
+        send_signals(relay, "inst", lax.rem(me + ni - 4, ni))
 
     def to_block(peer):
         return pltpu.make_async_remote_copy(
@@ -164,18 +180,27 @@
             send_sem=a_send, recv_sem=a_recv,
             device_id={"inst": other * 2 + cc}, device_id_type=MESH)
 
-    def others(act):
-        for k in far_first:
-            chosen = lax.rem(chip + k, nc)
-            act(chosen, 0)
-            act(chosen, 1)
-
+    def send_across():
+        for c in across:
+            for cc in range(2):
+                to_mixer(c, cc).start()
+
+    @pl.when(jnp.logical_not(lean))
+    def _():
+        send_across()
+
+    for c in beside:
         for cc in range(2):
-            @pl.when(core != cc)
-            def _():
-                act(chip, cc)
-
-    others(lambda c, cc: to_mixer(c, cc).start())
+            to_mixer(c, cc).start()
+    for cc in range(2):
+        @pl.when(core != cc)
+        def _():
+            to_mixer(chip, cc).start()
+
+    @pl.when(lean)
+    def _():
+        pl.semaphore_wait(relay, 1)
+        send_across()
 
     rest1.wait()
     rest2.wait()
@@ -373,7 +398,7 @@
                 vmem((2, nv, ny, nz), f32), vmem((2, nv, ny, nz), f32), vmem((nx, modes, nz), f32),
                 vmem((1, nz), f32), vmem((ns, 1, nz), f32),
                 sem((8,)), sem((9,)), sem, sem, sem, sem, sem((2,)), sem((2,)), sem, sem,
-                pltpu.SemaphoreType.REGULAR((ns,)),
+                pltpu.SemaphoreType.REGULAR((ns,)), pltpu.SemaphoreType.REGULAR,
             ],
             compiler_params=pltpu.CompilerParams(
                 collective_id=0, has_side_effects=True, vmem_limit_bytes=24 << 20),

time: 17.9 us -> 17.6 us (0.983)
  Pallas kernels: 17.1 us -> 16.9 us
    pallas_call x1, Pallas kernels: 16.5 us -> 16.2 us  [body(): pl.pallas_call(functools.partial(kernel, ni, ns), out_shape=(jax.ShapeDty...]
where the time goes in v9:
time: 17.6 us; the launch traced here: 17.5 us
  Pallas kernels  16.9 us (96%)
  between operations  0.64 us (4%)
    pallas_call x1, Pallas kernels, body(): pl.pallas_call(functools.partial(kernel, ni, ns), out_shape=(jax.ShapeDty...  16.2 us
    pallas_call x1, Pallas kernels, body(): pl.pallas_call(put_out, out_shape=(jax.ShapeDtypeStruct((1, nv, nx, ny, n...  0.69 us

profile of v9, /device:TPU:1, one launch (start us, length us, event | category | flops | bytes accessed | tf_op | source)
XLA Modules:
  0.0 17.5 jit_solution(10506996280793386942)
XLA Ops:
  0.6 16.2 %shard_map.104 = (f32[5,4,16,128]{3,2,1,0:T(8,128)S(1)}, f32[1,40]{1,0:T(1,128)S(1)}) custom-call(f32[1,5,4,16,128]{4,3,2,1,0:T(8,128)} %adj_hbm.1, f32[1,7,5,5,4,16,128]{6,5,4,3,2,1,0:T(8,128)} %jac_hbm.1, f32[4,16,128]{2,1,0:T(8,128)} %vol_hbm.1, f32[1,5,4,16,128]{4,3,2,1,0:T(8,128)} %src_hbm.1, f32[5,4,128]{2,1,0:T(4,128)} %so_hbm.1, ...), custom_call_target="tpu_custom_call" | custom-call | tf_op jit(solution)/shard_map/pallas_call | solution.py:387
  16.9 0.7 %shard_map.105 = (f32[1,5,4,16,128]{4,3,2,1,0:T(8,128)}, f32[1,40]{1,0:T(1,128)}) custom-call(f32[5,4,16,128]{3,2,1,0:T(8,128)S(1)} %get-tuple-element.4.res, f32[1,40]{1,0:T(1,128)S(1)} %get-tuple-element.5.modal), custom_call_target="tpu_custom_call" | custom-call | tf_op jit(solution)/shard_map/pallas_call | solution.py:406

commit v10 on v9

--- a/solution.py
+++ b/solution.py
@@ -160,17 +160,18 @@
 
     def halo(side):
         peer = lax.rem(sp + (1 if side == 0 else ns - 1), ns)
-        return peer, pltpu.make_async_remote_copy(
-            src_ref=halo_out.at[side], dst_ref=halo_in.at[side],
+        return peer, [pltpu.make_async_remote_copy(
+            src_ref=halo_out.at[side, j], dst_ref=halo_in.at[side, j],
             send_sem=h_send.at[side], recv_sem=h_recv.at[side],
-            device_id={"space": peer}, device_id_type=MESH)
+            device_id={"space": peer}, device_id_type=MESH) for j in range(nv)]
 
     for side in range(2):
-        target, copy = halo(side)
+        target, parts_of_halo = halo(side)
 
         @pl.when(turn(target) < my_turn)
         def _():
-            copy.start()
+            for copy in parts_of_halo:
+                copy.start()
 
     def to_mixer(other, cc):
         x, y = spot(other)
@@ -238,12 +239,13 @@
 
         later_blocks(act)
         for side in range(2):
-            target, copy = halo(side)
+            target, parts_of_halo = halo(side)
             chosen = is_near(target) if near else jnp.logical_not(is_near(target))
 
             @pl.when((turn(target) > my_turn) & chosen)
             def _():
-                copy.start()
+                for copy in parts_of_halo:
+                    copy.start()
 
     to_later(True)
 
@@ -314,8 +316,8 @@
                 res[j, x] = res[j, x] + vol[x] * mixed[j, x]
 
     def add_halo():
-        halo(0)[1].wait_recv()
-        halo(1)[1].wait_recv()
+        for side in range(2):
+            arrived(halo_in.at[side], h_recv.at[side])
         for j in range(nv):
             res[j, 0] = res[j, 0] + halo_in[0, j]
             res[j, nx - 1] = res[j, nx - 1] + halo_in[1, j]
@@ -345,8 +347,8 @@
         add_halo()
         add_mixed()
 
-    halo(0)[1].wait_send()
-    halo(1)[1].wait_send()
+    for side in range(2):
+        arrived(halo_out.at[side], h_send.at[side])
     for cc in range(2):
         @pl.when(core == cc)
         def _():
@@ -354,12 +356,17 @@
 
 
 def put_out(res, modal, res_hbm, modal_hbm, sem):
-    first = pltpu.make_async_copy(res, res_hbm.at[0], sem.at[0])
-    second = pltpu.make_async_copy(modal, modal_hbm, sem.at[1])
-    first.start()
-    second.start()
-    first.wait()
-    second.wait()
+    nv, nx = res.shape[:2]
+    half = nx // 2
+    copies = [pltpu.make_async_copy(modal, modal_hbm, sem.at[0])]
+    for j in range(nv):
+        for x in range(2):
+            part = pl.ds(x * half, half)
+            copies.append(pltpu.make_async_copy(res.at[j, part], res_hbm.at[0, j, part], sem.at[len(copies)]))
+    for copy in copies:
+        copy.start()
+    for copy in copies:
+        copy.wait()
 
 
 def solution(mesh):
@@ -408,7 +415,7 @@
             out_shape=(jax.ShapeDtypeStruct((1, nv, nx, ny, nz), f32), jax.ShapeDtypeStruct((1, modes), f32)),
             in_specs=[pl.BlockSpec(memory_space=vmem)] * 2,
             out_specs=(pl.BlockSpec(memory_space=pltpu.HBM), pl.BlockSpec(memory_space=pltpu.HBM)),
-            scratch_shapes=[sem((2,))],
+            scratch_shapes=[sem((1 + 2 * nv,))],
         )(*[pltpu.with_memory_space_constraint(x, vmem) for x in (residual, modal)])
 
     return jax.shard_map(

time: 17.6 us -> 17.7 us (level)
  no operation moved by 1% of the time
where the time goes in v10:
time: 17.7 us; the launch traced here: 17.6 us
  Pallas kernels  17 us (96%)
  between operations  0.64 us (4%)
    pallas_call x1, Pallas kernels, body(): pl.pallas_call(functools.partial(kernel, ni, ns), out_shape=(jax.ShapeDty...  16.2 us
    pallas_call x1, Pallas kernels, body(): pl.pallas_call(put_out, out_shape=(jax.ShapeDtypeStruct((1, nv, nx, ny, n...  0.76 us

profile of v10, /device:TPU:1, one launch (start us, length us, event | category | flops | bytes accessed | tf_op | source)
XLA Modules:
  0.0 17.6 jit_solution(6391850312298953810)
XLA Ops:
  0.6 16.2 %shard_map.104 = (f32[5,4,16,128]{3,2,1,0:T(8,128)S(1)}, f32[1,40]{1,0:T(1,128)S(1)}) custom-call(f32[1,5,4,16,128]{4,3,2,1,0:T(8,128)} %adj_hbm.1, f32[1,7,5,5,4,16,128]{6,5,4,3,2,1,0:T(8,128)} %jac_hbm.1, f32[4,16,128]{2,1,0:T(8,128)} %vol_hbm.1, f32[1,5,4,16,128]{4,3,2,1,0:T(8,128)} %src_hbm.1, f32[5,4,128]{2,1,0:T(4,128)} %so_hbm.1, ...), custom_call_target="tpu_custom_call" | custom-call | tf_op jit(solution)/shard_map/pallas_call | solution.py:394
  16.8 0.8 %shard_map.105 = (f32[1,5,4,16,128]{4,3,2,1,0:T(8,128)}, f32[1,40]{1,0:T(1,128)}) custom-call(f32[5,4,16,128]{3,2,1,0:T(8,128)S(1)} %get-tuple-element.4.res, f32[1,40]{1,0:T(1,128)S(1)} %get-tuple-element.5.modal), custom_call_target="tpu_custom_call" | custom-call | tf_op jit(solution)/shard_map/pallas_call | solution.py:413

commit v11 on v10

--- a/solution.py
+++ b/solution.py
@@ -356,17 +356,12 @@
 
 
 def put_out(res, modal, res_hbm, modal_hbm, sem):
-    nv, nx = res.shape[:2]
-    half = nx // 2
-    copies = [pltpu.make_async_copy(modal, modal_hbm, sem.at[0])]
-    for j in range(nv):
-        for x in range(2):
-            part = pl.ds(x * half, half)
-            copies.append(pltpu.make_async_copy(res.at[j, part], res_hbm.at[0, j, part], sem.at[len(copies)]))
-    for copy in copies:
-        copy.start()
-    for copy in copies:
-        copy.wait()
+    first = pltpu.make_async_copy(res, res_hbm.at[0], sem.at[0])
+    second = pltpu.make_async_copy(modal, modal_hbm, sem.at[1])
+    first.start()
+    second.start()
+    first.wait()
+    second.wait()
 
 
 def solution(mesh):
@@ -415,7 +410,7 @@
             out_shape=(jax.ShapeDtypeStruct((1, nv, nx, ny, nz), f32), jax.ShapeDtypeStruct((1, modes), f32)),
             in_specs=[pl.BlockSpec(memory_space=vmem)] * 2,
             out_specs=(pl.BlockSpec(memory_space=pltpu.HBM), pl.BlockSpec(memory_space=pltpu.HBM)),
-            scratch_shapes=[sem((1 + 2 * nv,))],
+            scratch_shapes=[sem((2,))],
         )(*[pltpu.with_memory_space_constraint(x, vmem) for x in (residual, modal)])
 
     return jax.shard_map(

time: 17.7 us -> 17.6 us (level)
  no operation moved by 1% of the time
where the time goes in v11:
time: 17.6 us; the launch traced here: 17.5 us
  Pallas kernels  16.9 us (96%)
  between operations  0.64 us (4%)
    pallas_call x1, Pallas kernels, body(): pl.pallas_call(functools.partial(kernel, ni, ns), out_shape=(jax.ShapeDty...  16.2 us
    pallas_call x1, Pallas kernels, body(): pl.pallas_call(put_out, out_shape=(jax.ShapeDtypeStruct((1, nv, nx, ny, n...  0.69 us

profile of v11, /device:TPU:1, one launch (start us, length us, event | category | flops | bytes accessed | tf_op | source)
XLA Modules:
  0.0 17.5 jit_solution(18214729720361117456)
XLA Ops:
  0.6 16.2 %shard_map.104 = (f32[5,4,16,128]{3,2,1,0:T(8,128)S(1)}, f32[1,40]{1,0:T(1,128)S(1)}) custom-call(f32[1,5,4,16,128]{4,3,2,1,0:T(8,128)} %adj_hbm.1, f32[1,7,5,5,4,16,128]{6,5,4,3,2,1,0:T(8,128)} %jac_hbm.1, f32[4,16,128]{2,1,0:T(8,128)} %vol_hbm.1, f32[1,5,4,16,128]{4,3,2,1,0:T(8,128)} %src_hbm.1, f32[5,4,128]{2,1,0:T(4,128)} %so_hbm.1, ...), custom_call_target="tpu_custom_call" | custom-call | tf_op jit(solution)/shard_map/pallas_call | solution.py:389
  16.8 0.7 %shard_map.105 = (f32[1,5,4,16,128]{4,3,2,1,0:T(8,128)}, f32[1,40]{1,0:T(1,128)}) custom-call(f32[5,4,16,128]{3,2,1,0:T(8,128)S(1)} %get-tuple-element.4.res, f32[1,40]{1,0:T(1,128)S(1)} %get-tuple-element.5.modal), custom_call_target="tpu_custom_call" | custom-call | tf_op jit(solution)/shard_map/pallas_call | solution.py:408

commit v12 on v11

--- a/solution.py
+++ b/solution.py
@@ -25,6 +25,7 @@
 
 LATE = 40
 LEAN = 71
+CLOSE = 55
 
 
 def turn(block):
@@ -69,24 +70,31 @@
     my_turn = turn(sp)
     lean = my_turn >= LEAN
 
-    @pl.when(jnp.logical_not(lean))
-    def _():
-        for c in across:
-            for cc in range(2):
-                send_signals(barrier, "inst", c * 2 + cc)
-
-    for c in beside:
-        for cc in range(2):
-            send_signals(barrier, "inst", c * 2 + cc)
-    send_signals(barrier, "inst", chip * 2 + 1 - core)
-
     def later_blocks(act):
         for peer in sorted(range(ns), key=turn_of):
             @pl.when(turn_of(peer) > my_turn)
             def _():
                 act(peer)
 
-    later_blocks(lambda peer: send_signals(barrier, "space", peer))
+    @pl.when(my_turn >= CLOSE)
+    def _():
+        later_blocks(lambda peer: send_signals(barrier, "space", peer))
+
+    @pl.when(jnp.logical_not(lean))
+    def _():
+        for c in across:
+            for cc in range(2):
+                send_signals(barrier, "inst", c * 2 + cc)
+
+    for c in beside:
+        for cc in range(2):
+            send_signals(barrier, "inst", c * 2 + cc)
+    send_signals(barrier, "inst", chip * 2 + 1 - core)
+
+    @pl.when(my_turn < CLOSE)
+    def _():
+        later_blocks(lambda peer: send_signals(barrier, "space", peer))
+
     n_earlier = sum(jnp.where(turn_of(p) < my_turn, 1, 0) for p in range(ns))
 
     small = [(st_hbm, st), (phi_hbm, phi), (so_hbm, so), (adj_hbm.at[0], adj), (inv_hbm, inv),
@@ -151,12 +159,15 @@
             send_sem=m_send, recv_sem=m_recv,
             device_id={"space": peer}, device_id_type=MESH)
 
-    for peer in sorted(range(ns), key=turn_of):
-        @pl.when(turn_of(peer) < my_turn)
-        def _():
-            to_block(peer).start()
-            send_signals(ready_space.at[sp], "space", peer)
-
+    def report(peers):
+        for peer in peers:
+            @pl.when(turn_of(peer) < my_turn)
+            def _():
+                to_block(peer).start()
+                send_signals(ready_space.at[sp], "space", peer)
+
+    in_turn = sorted(range(ns), key=turn_of)
+    report(in_turn[:1])
 
     def halo(side):
         peer = lax.rem(sp + (1 if side == 0 else ns - 1), ns)
@@ -172,6 +183,8 @@
         def _():
             for copy in parts_of_halo:
                 copy.start()
+
+    report(in_turn[1:])
 
     def to_mixer(other, cc):
         x, y = spot(other)

time: 17.6 us -> 17.6 us (level)
  no operation moved by 1% of the time
where the time goes in v12:
time: 17.6 us; the launch traced here: 17.5 us
  Pallas kernels  16.9 us (96%)
  between operations  0.64 us (4%)
    pallas_call x1, Pallas kernels, body(): pl.pallas_call(functools.partial(kernel, ni, ns), out_shape=(jax.ShapeDty...  16.2 us
    pallas_call x1, Pallas kernels, body(): pl.pallas_call(put_out, out_shape=(jax.ShapeDtypeStruct((1, nv, nx, ny, n...  0.69 us

profile of v12, /device:TPU:1, one launch (start us, length us, event | category | flops | bytes accessed | tf_op | source)
XLA Modules:
  0.0 17.5 jit_solution(16790386441600861640)
XLA Ops:
  0.6 16.2 %shard_map.104 = (f32[5,4,16,128]{3,2,1,0:T(8,128)S(1)}, f32[1,40]{1,0:T(1,128)S(1)}) custom-call(f32[1,5,4,16,128]{4,3,2,1,0:T(8,128)} %adj_hbm.1, f32[1,7,5,5,4,16,128]{6,5,4,3,2,1,0:T(8,128)} %jac_hbm.1, f32[4,16,128]{2,1,0:T(8,128)} %vol_hbm.1, f32[1,5,4,16,128]{4,3,2,1,0:T(8,128)} %src_hbm.1, f32[5,4,128]{2,1,0:T(4,128)} %so_hbm.1, ...), custom_call_target="tpu_custom_call" | custom-call | tf_op jit(solution)/shard_map/pallas_call | solution.py:402
  16.8 0.7 %shard_map.105 = (f32[1,5,4,16,128]{4,3,2,1,0:T(8,128)}, f32[1,40]{1,0:T(1,128)}) custom-call(f32[5,4,16,128]{3,2,1,0:T(8,128)S(1)} %get-tuple-element.4.res, f32[1,40]{1,0:T(1,128)S(1)} %get-tuple-element.5.modal), custom_call_target="tpu_custom_call" | custom-call | tf_op jit(solution)/shard_map/pallas_call | solution.py:421
